TPU v7x, 32 devices: a whole 2x2x4 slice. The times are simulated.
32 devices in a mesh: chan: 8 (over y, x, core), tm: 4 (over z).
Axes of the slice: x: 2, y: 2, z: 4, core: 2. Of those that a mesh axis runs over, the one named last changes fastest.
Arguments:
- traces: bfloat16 [1024, 8, 4096], P('chan', 'tm'), may hold values from -6 to 6
- pair_blocks: int32 [32, 2], P('chan'), may hold values from 0 to 7, as said below
- pair_count: int32 [8], P('chan'), may hold values from 1 to 4, as said below
Outputs:
- stacks: float32 [4096, 2048], P(('chan', 'tm'))
Inputs may be any that keep to these rules, and one draw needn't show every extreme that they name: `pair_blocks`: each owner's pairs use blocks at most 2 blocks away from the owner's own block index; the second block lies 1 to 4 blocks after the first; every owner's first slot pairs its lowest with its highest reachable block. `pair_count`: some owner has all slots live.
All inputs are finite; a program needn't handle non-finite values.
Results may differ from a plain program's by a relative error of at most 0.0052.
Values may be sent and summed in bfloat16 or wider, within the bound.
No kernel may reach another device: no remote copies, remote signals or barrier semaphores. Data moves between devices by JAX's collectives and lax.ppermute only.
A program may use at most 192 MiB of HBM per device.

v0:
```python
import functools
import math

import jax
import jax.numpy as jnp
import numpy as np
from jax import lax
from jax.experimental import pallas as pl
from jax.experimental.pallas import tpu as pltpu
from jax.sharding import PartitionSpec as P

NS = 4096
FB = 1024
F_LO = 64
LAGS = 2048
AXES = ("chan", "tm")

TURN = 4
QUARTER = NS // TURN
GROUP = FB // TURN
STEP = 32
INFO = 128
VMEM = 56 * 1024 * 1024


def bins():
    return np.concatenate([F_LO + g + TURN * np.arange(GROUP) for g in range(TURN)])


def wave(first, second):
    angle = 2.0 * np.pi * (np.multiply.outer(first, second) % NS) / NS
    return np.cos(angle).astype(np.float32), np.sin(angle).astype(np.float32)


def forward_seeds():
    coarse = wave(STEP * np.arange(QUARTER // STEP), bins())
    fine = wave(np.arange(STEP), bins())
    return coarse + fine


def inverse_seeds():
    lags = np.arange(LAGS // 2) - LAGS // 2
    coarse = wave(bins()[::STEP], lags)
    fine = wave(TURN * np.arange(STEP), lags)
    return coarse + fine


def turned(power, cosine, sine):
    return [
        ((1, cosine), (-1, sine)),
        ((-1, sine), (-1, cosine)),
        ((-1, cosine), (1, sine)),
        ((1, sine), (1, cosine)),
    ][power % 4]


def signed_sum(terms):
    total = None
    for sign, term in terms:
        if total is None:
            total = term if sign > 0 else -term
        else:
            total = total + term if sign > 0 else total - term
    return total


def forward_kernel(pairs, count, x, coarse_c, coarse_s, fine_c, fine_s, out, spec, table):
    rows = spec.shape[0]
    slots = pairs.shape[0]
    for g in range(TURN):
        columns = slice(g * GROUP, (g + 1) * GROUP)

        def fill(i, carry, columns=columns):
            c, s = coarse_c[pl.ds(i, 1), columns], coarse_s[pl.ds(i, 1), columns]
            fc, fs = fine_c[:, columns], fine_s[:, columns]
            at = pl.ds(pl.multiple_of(i * STEP, STEP), STEP)
            table[at, :GROUP] = (c * fc - s * fs).astype(jnp.bfloat16)
            table[at, GROUP:] = (s * fc + c * fs).astype(jnp.bfloat16)
            return carry

        lax.fori_loop(0, QUARTER // STEP, fill, 0, unroll=4)
        product = jnp.dot(x[...], table[...], preferred_element_type=jnp.float32)
        parts = [
            turned((F_LO + g) * m, product[m * rows : (m + 1) * rows, :GROUP], product[m * rows : (m + 1) * rows, GROUP:])
            for m in range(TURN)
        ]
        spec[:, columns] = signed_sum([p[0] for p in parts])
        spec[:, FB + g * GROUP : FB + (g + 1) * GROUP] = signed_sum([p[1] for p in parts])
    spectrum = spec[...]
    mean_power = jnp.sum(spectrum * spectrum, axis=1, keepdims=True) / FB
    out[:, : 2 * FB] = (spectrum * lax.rsqrt(mean_power + 1e-06)).astype(jnp.bfloat16)
    lane = lax.broadcasted_iota(jnp.int32, (rows, INFO), 1)
    info = jnp.where(lane == 2 * slots, count[0], 0)
    for slot in range(slots):
        for side in range(2):
            info = jnp.where(lane == 2 * slot + side, pairs[slot, side], info)
    out[:, 2 * FB :] = info.astype(jnp.float32).astype(jnp.bfloat16)


def forward(traces, pair_blocks, pair_count):
    rows = traces.shape[0] * traces.shape[1]
    samples = traces.reshape(rows, TURN, QUARTER).transpose(1, 0, 2).reshape(TURN * rows, QUARTER)
    smem = pl.BlockSpec(memory_space=pltpu.SMEM)
    vmem = pl.BlockSpec(memory_space=pltpu.VMEM)
    return pl.pallas_call(
        forward_kernel,
        out_shape=jax.ShapeDtypeStruct((rows, 2 * FB + INFO), jnp.bfloat16),
        in_specs=[smem, smem] + [vmem] * 5,
        out_specs=vmem,
        scratch_shapes=[pltpu.VMEM((rows, 2 * FB), jnp.float32), pltpu.VMEM((QUARTER, 2 * GROUP), jnp.bfloat16)],
        compiler_params=pltpu.CompilerParams(vmem_limit_bytes=VMEM),
        cost_estimate=pl.CostEstimate(
            flops=2 * rows * NS * 2 * FB, bytes_accessed=2 * rows * (NS + 2 * FB), transcendentals=0
        ),
        name="forward",
    )(pair_blocks, pair_count, samples, *forward_seeds())


def table_kernel(coarse_c, coarse_s, fine_c, fine_s, table_c, table_s):
    def fill(i, carry):
        c, s = coarse_c[pl.ds(i, 1), :], coarse_s[pl.ds(i, 1), :]
        at = pl.ds(pl.multiple_of(i * STEP, STEP), STEP)
        table_c[at, :] = (c * fine_c[...] - s * fine_s[...]).astype(jnp.bfloat16)
        table_s[at, :] = (s * fine_c[...] + c * fine_s[...]).astype(jnp.bfloat16)
        return carry

    lax.fori_loop(0, FB // STEP, fill, 0)


def inverse_tables():
    half = LAGS // 2
    vmem = pl.BlockSpec(memory_space=pltpu.VMEM)
    return pl.pallas_call(
        table_kernel,
        out_shape=[jax.ShapeDtypeStruct((FB, half), jnp.bfloat16)] * 2,
        in_specs=[vmem] * 4,
        out_specs=[vmem] * 2,
        compiler_params=pltpu.CompilerParams(vmem_limit_bytes=VMEM),
        cost_estimate=pl.CostEstimate(flops=8 * FB * half, bytes_accessed=4 * FB * half, transcendentals=0),
        name="inverse_tables",
    )(*inverse_seeds())


def cross_kernel(slots, groups, w, out, total, info_v, info_s, sem):
    owners = w.shape[0] // groups
    half = out.shape[1]
    for owner in range(owners):
        tail = w[owner * groups, :, 2 * half :].astype(jnp.float32)
        info_v[owner : owner + 1, :] = tail[:1, :].astype(jnp.int32)
    copy = pltpu.make_async_copy(info_v, info_s, sem)
    copy.start()
    copy.wait()
    lanes = 256

    def one(pair, carry):
        owner, slot = pair // slots, pair % slots
        first = pl.ds(info_s[owner, 2 * slot] * groups, groups)
        second = pl.ds(info_s[owner, 2 * slot + 1] * groups, groups)
        alive = slot < info_s[owner, 2 * slots]
        at_re = pl.ds(pl.multiple_of(pair * 16, 16), 8)
        at_im = pl.ds(pl.multiple_of(pair * 16 + 8, 8), 8)

        @pl.when(alive)
        def _():
            for offset in range(0, half, lanes):
                re = slice(offset, offset + lanes)
                im = slice(half + offset, half + offset + lanes)
                re_a, im_a = w[first, :, re].astype(jnp.float32), w[first, :, im].astype(jnp.float32)
                re_b, im_b = w[second, :, re].astype(jnp.float32), w[second, :, im].astype(jnp.float32)
                sum_re = jnp.sum(re_a * re_b + im_a * im_b, axis=0)
                sum_im = jnp.sum(im_a * re_b - re_a * im_b, axis=0)
                for k in range(0, lanes, 128):
                    total[(offset + k) // 128, at_re, :] = sum_re[:, k : k + 128]
                    total[(offset + k) // 128, at_im, :] = sum_im[:, k : k + 128]

        @pl.when(jnp.logical_not(alive))
        def _():
            for k in range(half // 128):
                total[k, at_re, :] = jnp.zeros((8, 128), jnp.float32)
                total[k, at_im, :] = jnp.zeros((8, 128), jnp.float32)

        return carry

    lax.fori_loop(0, owners * slots, one, 0)
    count = out.shape[0]
    for k in range(half // 128):
        even, odd = total[k, pl.ds(0, count, stride=2), :], total[k, pl.ds(1, count, stride=2), :]
        out[:, k * 128 : (k + 1) * 128] = (even + odd).astype(jnp.bfloat16)


def cross_fast(received, slots, groups):
    owners = received.shape[0] // groups
    half = (received.shape[2] - INFO) // 2
    vmem = pl.BlockSpec(memory_space=pltpu.VMEM)
    rows = owners * slots * 8
    return pl.pallas_call(
        functools.partial(cross_kernel, slots, groups),
        out_shape=jax.ShapeDtypeStruct((rows, half), jnp.bfloat16),
        in_specs=[vmem],
        out_specs=vmem,
        scratch_shapes=[
            pltpu.VMEM((half // 128, 2 * rows, 128), jnp.float32),
            pltpu.VMEM((owners, INFO), jnp.int32),
            pltpu.SMEM((owners, INFO), jnp.int32),
            pltpu.SemaphoreType.DMA,
        ],
        compiler_params=pltpu.CompilerParams(vmem_limit_bytes=VMEM),
        cost_estimate=pl.CostEstimate(
            flops=8 * rows * 8 * half, bytes_accessed=2 * received.size + 2 * rows * half, transcendentals=0
        ),
        name="cross",
    )(received)


def cross_plain(received, slots, groups, spans):
    half = (received.shape[2] - INFO) // 2
    owners = received.shape[0] // groups
    channels = received.shape[1] // spans
    info = received.reshape(owners, groups, -1, 2 * half + INFO)[:, 0, 0, 2 * half :].astype(jnp.int32)
    pairs = info[:, : 2 * slots].reshape(owners * slots, 2)
    alive = (lax.iota(jnp.int32, slots)[None, :] < info[:, 2 * slots][:, None]).astype(jnp.float32).reshape(-1)
    blocks = received[:, :, : 2 * half].reshape(owners, groups, channels, spans, 2, half)

    def one(inputs):
        pair, live = inputs
        first, second = blocks[pair[0]].astype(jnp.float32), blocks[pair[1]].astype(jnp.float32)
        re_a, im_a, re_b, im_b = first[..., 0, :], first[..., 1, :], second[..., 0, :], second[..., 1, :]
        cross_re = jnp.sum(re_a * re_b + im_a * im_b, axis=(0, 2))
        cross_im = jnp.sum(im_a * re_b - re_a * im_b, axis=(0, 2))
        return (jnp.stack([cross_re, cross_im]) * live).astype(jnp.bfloat16)

    return lax.map(one, (pairs, alive))


def inverse_kernel(scale, y, table_c, table_s, out):
    rows = y.shape[0]
    half = LAGS // 2
    target = lax.broadcasted_iota(jnp.int32, (rows, rows), 0)
    source = lax.broadcasted_iota(jnp.int32, (rows, rows), 1)
    wanted = source // 8 * 4 + source % 4 + source // 4 % 2 * (rows // 2)
    pick = jnp.where(target == wanted, 1.0, 0.0).astype(jnp.bfloat16)
    ordered = jnp.dot(pick, y[...], preferred_element_type=jnp.float32).astype(jnp.bfloat16)
    near, far = [], []
    for g in range(TURN):
        columns = slice(g * GROUP, (g + 1) * GROUP)
        by_c = jnp.dot(ordered[:, columns], table_c[columns, :], preferred_element_type=jnp.float32)
        by_s = jnp.dot(ordered[:, columns], table_s[columns, :], preferred_element_type=jnp.float32)
        straight = by_c[: rows // 2] - by_s[rows // 2 :]
        crossed = by_s[: rows // 2] + by_c[rows // 2 :]
        near.append((1, straight))
        far.append([(1, straight), (-1, crossed), (-1, straight), (1, crossed)][(F_LO + g) % 4])
    out[:, :half] = signed_sum(near) * scale
    out[:, half:] = signed_sum(far) * scale


def inverse(y, table_c, table_s, scale):
    rows = y.shape[0]
    vmem = pl.BlockSpec(memory_space=pltpu.VMEM)
    return pl.pallas_call(
        functools.partial(inverse_kernel, scale),
        out_shape=jax.ShapeDtypeStruct((rows // 2, LAGS), jnp.float32),
        in_specs=[vmem] * 3,
        out_specs=vmem,
        compiler_params=pltpu.CompilerParams(vmem_limit_bytes=VMEM),
        cost_estimate=pl.CostEstimate(
            flops=2 * rows * FB * LAGS, bytes_accessed=2 * FB * LAGS + 2 * rows * LAGS, transcendentals=0
        ),
        name="inverse",
    )(y, table_c, table_s)


def on_device(traces, pair_blocks, pair_count):
    owners, groups = lax.axis_size("chan"), lax.axis_size("tm")
    devices = owners * groups
    block, spans = traces.shape[0], traces.shape[1]
    slots = pair_blocks.shape[0]
    pieces = groups // slots
    channel_parts = min(devices, block // pieces)
    bin_parts = devices // channel_parts
    channels = block // pieces // channel_parts
    bin_share = FB // bin_parts
    scale = 1.0 / math.sqrt(FB * spans * groups)

    white = forward(traces, pair_blocks, pair_count)
    table_c, table_s = inverse_tables()
    simple = pieces == 1 and bin_parts == 1
    if simple:
        sent = white.reshape(devices, channels * spans, 2 * FB + INFO)
    else:
        body = white[:, : 2 * FB].reshape(pieces, channel_parts, channels, spans, 2, bin_parts, bin_share)
        body = body.transpose(1, 5, 0, 2, 3, 4, 6).reshape(devices, pieces * channels * spans, 2 * bin_share)
        tail = jnp.broadcast_to(white[:1, 2 * FB :], body.shape[:2] + (INFO,))
        sent = jnp.concatenate([body, tail], axis=2)
    received = lax.all_to_all(sent, AXES, split_axis=0, concat_axis=0, tiled=True)
    if simple and channels * spans == 8 and spans == 2:
        cross = cross_fast(received, slots, groups).reshape(devices, 8, FB)
    else:
        cross = cross_plain(received, slots, groups, spans)
        cross = cross.reshape(owners, slots, 2, pieces, channels, bin_share).transpose(0, 1, 3, 2, 4, 5)
        cross = cross.reshape(devices, 2 * channels, bin_share)
    own = lax.all_to_all(cross, AXES, split_axis=0, concat_axis=0, tiled=True)
    rows = block // pieces
    if not (simple and channels == 4):
        own = own.reshape(channel_parts, bin_parts, 2, channels, bin_share).transpose(0, 3, 2, 1, 4)
        own = own.reshape(rows // 4, 4, 2, FB).transpose(0, 2, 1, 3)
    return inverse(own.reshape(2 * rows, FB), table_c, table_s, scale)


def solution(mesh):
    return jax.shard_map(
        on_device,
        mesh=mesh,
        in_specs=(P("chan", "tm", None), P("chan", None), P("chan")),
        out_specs=P(("chan", "tm"), None),
        check_vma=False,
    )
```

profile of v0, /device:TPU:1, one launch (start us, length us, event | category | flops | bytes accessed | tf_op | source)
XLA Modules:
  0.0 85.3 jit_solution(2043585823381425464)
XLA Ops:
  0.7 1.3 %copy.13.pairs = s32[4,2]{1,0:T(4,128)} copy(s32[4,2]{0,1:T(2,128)} %param.12) | data formatting | bytes 64 | tf_op args[1]
  2.0 3.1 %reshape.15 = bf16[256,4,1024]{2,1,0:T(4,128)(2,1)S(1)} reshape(bf16[128,2,4096]{2,1,0:T(2,128)(2,1)} %param.11) | data formatting | bytes 4194304 | tf_op jit(solution)/shard_map/reshape | solution.py:102
  5.1 2.0 %copy.12 = bf16[256,4,1024]{2,0,1:T(8,128)(2,1)} copy(bf16[256,4,1024]{2,1,0:T(4,128)(2,1)S(1)} %reshape.15) | data formatting | bytes 4194304 | tf_op jit(solution)/shard_map/reshape | solution.py:102
  7.1 13.5 %forward.1 = bf16[256,2176]{1,0:T(8,128)(2,1)} custom-call(s32[4,2]{1,0:T(4,128)} %copy.13.pairs, s32[1]{0:T(128)S(6)} %copy.14.count, bf16[1024,1024]{1,0:T(8,128)(2,1)} %bitcast.7, f32[32,1024]{1,0:T(8,128)} %constant.16.clone.coarse_c, f32[32,1024]{1,0:T(8,128)} %constant.17.clone.coarse_s, f32[32,1024]{1,0:T(8,128)} %constant.18.clone.fine_c, ...), custom_call_target="tpu_custom_call" | custom-call | flops 4294967296 | bytes 3145728 | tf_op jit(solution)/shard_map/forward/pallas_call | solution.py:105
  20.6 36.2 %all_to_all.10.w = bf16[32,8,2176]{2,1,0:T(8,128)(2,1)} all-to-all(bf16[32,8,2176]{2,1,0:T(8,128)(2,1)} %bitcast.9), channel_id=1, replica_groups=mesh['chan'=8,'tm'=4] {'chan','tm'}, dimensions={0} | all-to-all | bytes 2228224 | tf_op jit(solution)/shard_map/all_to_all | solution.py:294
  56.8 4.8 %cross.1 = bf16[256,1024]{1,0:T(8,128)(2,1)} custom-call(bf16[32,8,2176]{2,1,0:T(8,128)(2,1)} %all_to_all.10.w), custom_call_target="tpu_custom_call" | custom-call | flops 16777216 | bytes 1638400 | tf_op jit(solution)/shard_map/cross/pallas_call | solution.py:196
  61.6 2.6 %all-to-all-start.1 = ((bf16[32,8,1024]{2,1,0:T(8,128)(2,1)}), bf16[32,8,1024]{2,1,0:T(8,128)(2,1)S(1)}, u32[]{:S(2)}, u32[]{:S(2)}) async-start(bf16[32,8,1024]{2,1,0:T(8,128)(2,1)} %bitcast.6), calls=%async_computation.1 | async-start | bytes 1048576 | tf_op jit(solution)/shard_map/all_to_all | solution.py:301
  64.2 4.4 %inverse_tables.1 = (bf16[1024,1024]{1,0:T(8,128)(2,1)}, bf16[1024,1024]{1,0:T(8,128)(2,1)}) custom-call(f32[32,1024]{1,0:T(8,128)} %constant.20.clone.coarse_c, f32[32,1024]{1,0:T(8,128)} %constant.21.clone.coarse_s, f32[32,1024]{1,0:T(8,128)} %constant.22.clone.fine_c, f32[32,1024]{1,0:T(8,128)} %constant.23.clone.fine_s), custom_call_target="tpu_custom_call" | custom-call | flops 8388608 | bytes 4194304 | tf_op jit(solution)/shard_map/inverse_tables/pallas_call | solution.py:133
  68.6 11.1 %all-to-all-done.1 = bf16[32,8,1024]{2,1,0:T(8,128)(2,1)S(1)} async-done(((bf16[32,8,1024]{2,1,0:T(8,128)(2,1)}), bf16[32,8,1024]{2,1,0:T(8,128)(2,1)S(1)}, u32[]{:S(2)}, u32[]{:S(2)}) %all-to-all-start.1) | async-done | bytes 524320 | tf_op jit(solution)/shard_map/all_to_all | solution.py:301
  79.7 0.0 copy-start
  79.7 0.8 copy-done
  80.5 4.9 %inverse.1 = f32[128,2048]{1,0:T(8,128)} custom-call(bf16[256,1024]{1,0:T(8,128)(2,1)} %bitcast.8, bf16[1024,1024]{1,0:T(8,128)(2,1)} %get-tuple-element.7.table_c, bf16[1024,1024]{1,0:T(8,128)(2,1)} %get-tuple-element.8.table_s), custom_call_target="tpu_custom_call" | custom-call | flops 1073741824 | bytes 5242880 | tf_op jit(solution)/shard_map/inverse/pallas_call | solution.py:259
Async XLA Ops:
  61.6 18.1 %all-to-all-start.1 = ((bf16[32,8,1024]{2,1,0:T(8,128)(2,1)}), bf16[32,8,1024]{2,1,0:T(8,128)(2,1)S(1)}, u32[]{:S(2)}, u32[]{:S(2)}) async-start(bf16[32,8,1024]{2,1,0:T(8,128)(2,1)} %bitcast.6), calls=%async_computation.1 | async-start | bytes 1048576 | tf_op jit(solution)/shard_map/all_to_all | solution.py:301
  79.7 0.8 copy-start
where the time goes:
time: 85.9 us; the launch traced here: 85.3 us
  blocking collectives  36.2 us (42%)
  Pallas kernels  27.5 us (32%)
  waiting for transfers between devices  11.1 us (13%)
  local copies, waits for them, and re-layouts  7.25 us (8%)
  starting transfers between devices  2.62 us (3%)
    all_to_all x1, blocking collectives, on_device(): lax.all_to_all(sent, AXES, split_axis=0, concat_axis=0, tiled=True)  36.2 us
    pallas_call x1, Pallas kernels, forward(): pl.pallas_call(forward_kernel, out_shape=jax.ShapeDtypeStruct((rows, 2 *...  13.5 us
    all_to_all x1, waiting for transfers between devices, on_device(): own = lax.all_to_all(cross, AXES, split_axis=0, concat_axis=0, tiled=True)  11.1 us
    reshape x2, local copies, waits for them, and re-layouts, forward(): traces.reshape(rows, TURN, QUARTER).transpose(1, 0, 2)  5.11 us
    pallas_call x1, Pallas kernels, inverse(): pl.pallas_call(functools.partial(inverse_kernel, scale), out_shape=jax.Sh...  4.86 us
    pallas_call x1, Pallas kernels, cross_fast(): pl.pallas_call(functools.partial(cross_kernel, slots, groups), out_shape=...  4.76 us
    pallas_call x1, Pallas kernels, inverse_tables(): pl.pallas_call(table_kernel, out_shape=[jax.ShapeDtypeStruct((FB, half),...  4.35 us
    all_to_all x1, starting transfers between devices, on_device(): own = lax.all_to_all(cross, AXES, split_axis=0, concat_axis=0, tiled=True)  2.62 us
  transfers between devices with their start and end apart: 1, of which 1 were waited for; matrix products, arithmetic and copies ran while one was open for 0% of the time, Pallas kernels for 5%

commit v1 on v0

v1 whole, which is shorter than its diff:
```python
import functools
import math

import jax
import jax.numpy as jnp
import numpy as np
from jax import lax
from jax.experimental import pallas as pl
from jax.experimental.pallas import tpu as pltpu
from jax.sharding import PartitionSpec as P

NS = 4096
FB = 1024
F_LO = 64
LAGS = 2048
AXES = ("chan", "tm")

TURN = 4
QUARTER = NS // TURN
GROUP = FB // TURN
STEP = 32
VMEM = 24 * 1024 * 1024


def bins():
    return np.concatenate([F_LO + g + TURN * np.arange(GROUP) for g in range(TURN)])


def wave(first, second):
    angle = 2.0 * np.pi * (np.multiply.outer(first, second) % NS) / NS
    return np.cos(angle).astype(np.float32), np.sin(angle).astype(np.float32)


def forward_seeds():
    coarse = wave(STEP * np.arange(QUARTER // STEP), bins())
    fine = wave(np.arange(STEP), bins())
    return np.concatenate(coarse + fine)


def inverse_seeds():
    lags = np.arange(LAGS // 2) - LAGS // 2
    coarse = wave(bins()[::STEP], lags)
    fine = wave(TURN * np.arange(STEP), lags)
    return np.concatenate(coarse + fine)


def forward_kernel(x_hbm, seeds_hbm, out, x, seeds, spec, table, plus, minus, sems):
    rows = spec.shape[0]
    seed_copy = pltpu.make_async_copy(seeds_hbm, seeds, sems.at[0])
    x_copy = pltpu.make_async_copy(x_hbm, x, sems.at[1])
    seed_copy.start()
    x_copy.start()
    seed_copy.wait()
    coarse = QUARTER // STEP
    for g in range(TURN):
        columns = slice(g * GROUP, (g + 1) * GROUP)
        cosine, sine = table.at[g % 2, :, :GROUP], table.at[g % 2, :, GROUP:]
        for i in range(coarse):
            c, s = seeds[i : i + 1, columns], seeds[coarse + i : coarse + i + 1, columns]
            fc, fs = seeds[2 * coarse : 2 * coarse + STEP, columns], seeds[2 * coarse + STEP :, columns]
            at = slice(i * STEP, (i + 1) * STEP)
            cosine[at, :] = (c * fc - s * fs).astype(jnp.bfloat16)
            sine[at, :] = -(s * fc + c * fs).astype(jnp.bfloat16)
        if g == 0:
            x_copy.wait()
            for m in range(TURN):
                samples = slice(m * QUARTER, (m + 1) * QUARTER)
                quarter = x[:, :, samples].reshape(rows, QUARTER)
                plus[:, samples] = quarter
                minus[:, samples] = -quarter
        phases = [(F_LO + g) * m % 4 for m in range(TURN)]
        real = [[(1, cosine), (1, sine), (-1, cosine), (-1, sine)][p] for p in phases]
        imag = [[(1, sine), (-1, cosine), (-1, sine), (1, cosine)][p] for p in phases]
        for start, terms in ((0, real), (FB, imag)):
            left = [
                (plus if sign > 0 else minus)[:, m * QUARTER : (m + 1) * QUARTER] for m, (sign, _) in enumerate(terms)
            ]
            right = [half[...] for _, half in terms]
            spec[:, start + g * GROUP : start + (g + 1) * GROUP] = jnp.dot(
                jnp.concatenate(left, axis=1), jnp.concatenate(right, axis=0), preferred_element_type=jnp.float32
            )
    spectrum = spec[...]
    mean_power = jnp.sum(spectrum * spectrum, axis=1, keepdims=True) / FB
    out[...] = (spectrum * lax.rsqrt(mean_power + 1e-06)).astype(jnp.bfloat16)


def in_hbm(array):
    return pltpu.with_memory_space_constraint(array, pltpu.HBM)


def forward(traces):
    rows = traces.shape[0] * traces.shape[1]
    seeds = forward_seeds()
    return pl.pallas_call(
        forward_kernel,
        out_shape=jax.ShapeDtypeStruct((rows, 2 * FB), jnp.bfloat16),
        in_specs=[pl.BlockSpec(memory_space=pltpu.HBM)] * 2,
        out_specs=pl.BlockSpec(memory_space=pltpu.VMEM),
        scratch_shapes=[
            pltpu.VMEM(traces.shape, jnp.bfloat16),
            pltpu.VMEM(seeds.shape, jnp.float32),
            pltpu.VMEM((rows, 2 * FB), jnp.float32),
            pltpu.VMEM((2, QUARTER, 2 * GROUP), jnp.bfloat16),
            pltpu.VMEM((rows, NS), jnp.bfloat16),
            pltpu.VMEM((rows, NS), jnp.bfloat16),
            pltpu.SemaphoreType.DMA((2,)),
        ],
        compiler_params=pltpu.CompilerParams(vmem_limit_bytes=VMEM),
        cost_estimate=pl.CostEstimate(
            flops=2 * rows * NS * 2 * FB, bytes_accessed=2 * rows * (NS + 2 * FB), transcendentals=0
        ),
        name="forward",
    )(in_hbm(traces), in_hbm(jnp.asarray(seeds)))


def cross_kernel(slots, groups, info, w, out, total):
    owners = w.shape[0] // groups
    half = out.shape[1]
    lanes = 256

    def one(pair, carry):
        owner, slot = pair // slots, pair % slots
        first = pl.ds(info[owner, 2 * slot] * groups, groups)
        second = pl.ds(info[owner, 2 * slot + 1] * groups, groups)
        alive = slot < info[owner, 2 * slots]
        at_re = pl.ds(pl.multiple_of(pair * 16, 16), 8)
        at_im = pl.ds(pl.multiple_of(pair * 16 + 8, 8), 8)

        @pl.when(alive)
        def _():
            for offset in range(0, half, lanes):
                re = slice(offset, offset + lanes)
                im = slice(half + offset, half + offset + lanes)
                re_a, im_a = w[first, :, re].astype(jnp.float32), w[first, :, im].astype(jnp.float32)
                re_b, im_b = w[second, :, re].astype(jnp.float32), w[second, :, im].astype(jnp.float32)
                sum_re = jnp.sum(re_a * re_b + im_a * im_b, axis=0)
                sum_im = jnp.sum(im_a * re_b - re_a * im_b, axis=0)
                for k in range(0, lanes, 128):
                    total[(offset + k) // 128, at_re, :] = sum_re[:, k : k + 128]
                    total[(offset + k) // 128, at_im, :] = sum_im[:, k : k + 128]

        @pl.when(jnp.logical_not(alive))
        def _():
            for k in range(half // 128):
                total[k, at_re, :] = jnp.zeros((8, 128), jnp.float32)
                total[k, at_im, :] = jnp.zeros((8, 128), jnp.float32)

        return carry

    lax.fori_loop(0, owners * slots, one, 0)
    count = out.shape[0]
    for k in range(half // 128):
        even, odd = total[k, pl.ds(0, count, stride=2), :], total[k, pl.ds(1, count, stride=2), :]
        out[:, k * 128 : (k + 1) * 128] = (even + odd).astype(jnp.bfloat16)


def cross_fast(received, info, slots, groups):
    owners = received.shape[0] // groups
    half = received.shape[2] // 2
    vmem = pl.BlockSpec(memory_space=pltpu.VMEM)
    rows = owners * slots * 8
    return pl.pallas_call(
        functools.partial(cross_kernel, slots, groups),
        out_shape=jax.ShapeDtypeStruct((rows, half), jnp.bfloat16),
        in_specs=[pl.BlockSpec(memory_space=pltpu.SMEM), vmem],
        out_specs=vmem,
        scratch_shapes=[pltpu.VMEM((half // 128, 2 * rows, 128), jnp.float32)],
        compiler_params=pltpu.CompilerParams(vmem_limit_bytes=VMEM),
        cost_estimate=pl.CostEstimate(
            flops=8 * rows * 8 * half, bytes_accessed=2 * received.size + 2 * rows * half, transcendentals=0
        ),
        name="cross",
    )(info, received)


def cross_plain(received, info, slots, groups, spans):
    half = received.shape[2] // 2
    owners = received.shape[0] // groups
    channels = received.shape[1] // spans
    pairs = info[:, : 2 * slots].reshape(owners * slots, 2)
    alive = (lax.iota(jnp.int32, slots)[None, :] < info[:, 2 * slots][:, None]).astype(jnp.float32).reshape(-1)
    blocks = received.reshape(owners, groups, channels, spans, 2, half)

    def one(inputs):
        pair, live = inputs
        first, second = blocks[pair[0]].astype(jnp.float32), blocks[pair[1]].astype(jnp.float32)
        re_a, im_a, re_b, im_b = first[..., 0, :], first[..., 1, :], second[..., 0, :], second[..., 1, :]
        cross_re = jnp.sum(re_a * re_b + im_a * im_b, axis=(0, 2))
        cross_im = jnp.sum(im_a * re_b - re_a * im_b, axis=(0, 2))
        return (jnp.stack([cross_re, cross_im]) * live).astype(jnp.bfloat16)

    return lax.map(one, (pairs, alive))


def every_owner(row):
    owners = lax.axis_size("chan")
    ring = row
    while ring.shape[0] < owners:
        hop = ring.shape[0]
        more = lax.ppermute(ring, "chan", [(source, (source - hop) % owners) for source in range(owners)])
        ring = jnp.concatenate([ring, more])[:owners]
    return jnp.roll(ring, lax.axis_index("chan"), axis=0)


def inverse_kernel(scale, y, seeds, out_hbm, out, ordered, table, sem):
    rows = y.shape[0]
    half = LAGS // 2
    coarse = FB // STEP
    lanes = 256
    target = lax.broadcasted_iota(jnp.int32, (rows, rows), 0)
    source = lax.broadcasted_iota(jnp.int32, (rows, rows), 1)
    channel, part = source // 8 * 4 + source % 4, source // 4 % 2
    first = (target < rows // 2) & (target == channel)
    second = target == channel + rows // 2
    for g in range(TURN):
        columns = slice(g * GROUP, (g + 1) * GROUP)
        sign, swap = [(1, 0), (-1, 1), (-1, 0), (1, 1)][(F_LO + g) % 4]
        for meets in range(2):
            turned = (-sign if swap and meets else sign) * jnp.where(part == (meets ^ swap), 1.0, 0.0)
            pick = jnp.where(first, jnp.where(part == meets, 1.0, 0.0), jnp.where(second, turned, 0.0))
            ordered[:, meets * FB + g * GROUP : meets * FB + (g + 1) * GROUP] = jnp.dot(
                pick.astype(jnp.bfloat16), y[:, columns], preferred_element_type=jnp.float32
            ).astype(jnp.bfloat16)
    copies = []
    for k, offset in enumerate(range(0, half, lanes)):
        columns = slice(offset, offset + lanes)
        fc, fs = seeds[2 * coarse : 2 * coarse + STEP, columns], seeds[2 * coarse + STEP :, columns]
        for i in range(coarse):
            c, s = seeds[i : i + 1, columns], seeds[coarse + i : coarse + i + 1, columns]
            table[k % 2, i * STEP : (i + 1) * STEP, :] = (c * fc - s * fs).astype(jnp.bfloat16)
            table[k % 2, FB + i * STEP : FB + (i + 1) * STEP, :] = -(s * fc + c * fs).astype(jnp.bfloat16)
        product = jnp.dot(ordered[...], table[k % 2], preferred_element_type=jnp.float32) * scale
        for side in range(2):
            at = slice(side * half + offset, side * half + offset + lanes)
            out[:, at] = product[side * rows // 2 : (side + 1) * rows // 2]
            copies.append(pltpu.make_async_copy(out.at[:, at], out_hbm.at[:, at], sem.at[2 * k + side]))
            copies[-1].start()
    for copy in copies:
        copy.wait()


def inverse(y, scale):
    rows = y.shape[0]
    seeds = inverse_seeds()
    vmem = pl.BlockSpec(memory_space=pltpu.VMEM)
    return pl.pallas_call(
        functools.partial(inverse_kernel, scale),
        out_shape=jax.ShapeDtypeStruct((rows // 2, LAGS), jnp.float32),
        in_specs=[vmem] * 2,
        out_specs=pl.BlockSpec(memory_space=pltpu.HBM),
        scratch_shapes=[
            pltpu.VMEM((rows // 2, LAGS), jnp.float32),
            pltpu.VMEM((rows, 2 * FB), jnp.bfloat16),
            pltpu.VMEM((2, 2 * FB, 256), jnp.bfloat16),
            pltpu.SemaphoreType.DMA((LAGS // 256,)),
        ],
        compiler_params=pltpu.CompilerParams(vmem_limit_bytes=VMEM),
        cost_estimate=pl.CostEstimate(
            flops=2 * rows * FB * LAGS, bytes_accessed=2 * rows * FB + 2 * rows * LAGS, transcendentals=0
        ),
        name="inverse",
    )(y, jnp.asarray(seeds))


def on_device(traces, pair_blocks, pair_count):
    owners, groups = lax.axis_size("chan"), lax.axis_size("tm")
    devices = owners * groups
    block, spans = traces.shape[0], traces.shape[1]
    slots = pair_blocks.shape[0]
    pieces = groups // slots
    channel_parts = min(devices, block // pieces)
    bin_parts = devices // channel_parts
    channels = block // pieces // channel_parts
    bin_share = FB // bin_parts
    scale = 1.0 / math.sqrt(FB * spans * groups)

    white = forward(traces)
    simple = pieces == 1 and bin_parts == 1
    if simple:
        sent = white.reshape(devices, channels * spans, 2 * FB)
    else:
        sent = white.reshape(pieces, channel_parts, channels, spans, 2, bin_parts, bin_share)
        sent = sent.transpose(1, 5, 0, 2, 3, 4, 6).reshape(devices, pieces * channels * spans, 2 * bin_share)
    received = lax.all_to_all(sent, AXES, split_axis=0, concat_axis=0, tiled=True)
    row = jnp.concatenate([pair_blocks.reshape(1, 2 * slots), pair_count.reshape(1, 1)], axis=1)
    info = every_owner(lax.optimization_barrier((row, white))[0])
    if simple and channels * spans == 8 and spans == 2:
        cross = cross_fast(received, info, slots, groups).reshape(devices, 8, FB)
    else:
        cross = cross_plain(received, info, slots, groups, spans)
        cross = cross.reshape(owners, slots, 2, pieces, channels, bin_share).transpose(0, 1, 3, 2, 4, 5)
        cross = cross.reshape(devices, 2 * channels, bin_share)
    own = lax.all_to_all(cross, AXES, split_axis=0, concat_axis=0, tiled=True)
    rows = block // pieces
    if not (simple and channels == 4):
        own = own.reshape(channel_parts, bin_parts, 2, channels, bin_share).transpose(0, 3, 2, 1, 4)
        own = own.reshape(rows // 4, 4, 2, FB).transpose(0, 2, 1, 3)
    return inverse(own.reshape(2 * rows, FB), scale)


def solution(mesh):
    return jax.shard_map(
        on_device,
        mesh=mesh,
        in_specs=(P("chan", "tm", None), P("chan", None), P("chan")),
        out_specs=P(("chan", "tm"), None),
        check_vma=False,
    )
```

time: 85.9 us -> 65.3 us (0.76)
  blocking collectives: 36.2 us -> 18.3 us
  Pallas kernels: 27.5 us -> 13.3 us
  waiting for transfers between devices: 11.1 us -> 23.6 us
  local copies, waits for them, and re-layouts: 7.25 us -> 0.24 us
  starting transfers between devices: 2.62 us -> 8.85 us
    all_to_all x1, blocking collectives: 36.2 us -> 18.3 us  [on_device(): own = lax.all_to_all(cross, AXES, split_axis=0, concat_axis=0, tiled=True)]
    ppermute x0 -> x3, waiting for transfers between devices: none -> 10.4 us  [every_owner(): lax.ppermute(ring, 'chan', [(source, (source - hop) % owners) for source...]
    pallas_call x1, Pallas kernels: 13.5 us -> 8.01 us  [forward(): pl.pallas_call(forward_kernel, out_shape=jax.ShapeDtypeStruct((rows, 2 *...]
    reshape x2 -> x1, local copies, waits for them, and re-layouts: 5.11 us -> 0.09 us  [on_device(): pair_blocks.reshape(1, 2 * slots)]
    all_to_all x1, starting transfers between devices: 2.62 us -> 7.1 us  [on_device(): lax.all_to_all(sent, AXES, split_axis=0, concat_axis=0, tiled=True)]
    pallas_call x1 -> x0, Pallas kernels: 4.35 us -> none  [inverse_tables(): pl.pallas_call(table_kernel, out_shape=[jax.ShapeDtypeStruct((FB, half),...]
    pallas_call x1, Pallas kernels: 4.86 us -> 2.56 us  [inverse(): pl.pallas_call(functools.partial(inverse_kernel, scale), out_shape=jax.Sh...]
    all_to_all x1, waiting for transfers between devices: 11.1 us -> 13.2 us  [on_device(): lax.all_to_all(sent, AXES, split_axis=0, concat_axis=0, tiled=True)]
  transfers between devices with their start and end apart: 1 -> 4, of which waited for: 1 -> 4; matrix products, arithmetic and copies ran while one was open for 0% -> 0% of each run, Pallas kernels for 5% -> 0%
where the time goes in v1:
time: 65.3 us; the launch traced here: 65.1 us
  waiting for transfers between devices  23.6 us (36%)
  blocking collectives  18.3 us (28%)
  Pallas kernels  13.3 us (20%)
  starting transfers between devices  8.85 us (14%)
  between operations  0.71 us (1%)
    all_to_all x1, blocking collectives, on_device(): own = lax.all_to_all(cross, AXES, split_axis=0, concat_axis=0, tiled=True)  18.3 us
    all_to_all x1, waiting for transfers between devices, on_device(): lax.all_to_all(sent, AXES, split_axis=0, concat_axis=0, tiled=True)  13.2 us
    ppermute x3, waiting for transfers between devices, every_owner(): lax.ppermute(ring, 'chan', [(source, (source - hop) % owners) for source...  10.4 us
    pallas_call x1, Pallas kernels, forward(): pl.pallas_call(forward_kernel, out_shape=jax.ShapeDtypeStruct((rows, 2 *...  8.01 us
    all_to_all x1, starting transfers between devices, on_device(): lax.all_to_all(sent, AXES, split_axis=0, concat_axis=0, tiled=True)  7.1 us
    pallas_call x1, Pallas kernels, cross_fast(): pl.pallas_call(functools.partial(cross_kernel, slots, groups), out_shape=...  2.73 us
    pallas_call x1, Pallas kernels, inverse(): pl.pallas_call(functools.partial(inverse_kernel, scale), out_shape=jax.Sh...  2.56 us
    ppermute x3, starting transfers between devices, every_owner(): lax.ppermute(ring, 'chan', [(source, (source - hop) % owners) for source...  1.76 us
  transfers between devices with their start and end apart: 4, of which 4 were waited for; matrix products, arithmetic and copies ran while one was open for 0% of the time, Pallas kernels for 0%

profile of v1, /device:TPU:1, one launch (start us, length us, event | category | flops | bytes accessed | tf_op | source)
XLA Modules:
  0.0 65.1 jit_solution(8081434586565013101)
XLA Ops:
  0.0 8.0 %forward.1 = bf16[256,2048]{1,0:T(8,128)(2,1)} custom-call(bf16[128,2,4096]{2,1,0:T(2,128)(2,1)} %x_hbm.1, f32[128,1024]{1,0:T(8,128)} %constant.32.clone.seeds_hbm), custom_call_target="tpu_custom_call" | custom-call | flops 4294967296 | bytes 3145728 | tf_op jit(solution)/shard_map/forward/pallas_call | solution.py:94
  8.0 0.0 copy-start.1
  8.0 0.0 copy-start
  8.0 7.1 %all-to-all-start = ((bf16[32,8,2048]{2,1,0:T(8,128)(2,1)}), bf16[32,8,2048]{2,1,0:T(8,128)(2,1)S(1)}, u32[]{:S(2)}, u32[]{:S(2)}) async-start(bf16[32,8,2048]{2,1,0:T(8,128)(2,1)} %bitcast.1), calls=%async_computation | async-start | bytes 2097152 | tf_op jit(solution)/shard_map/all_to_all | solution.py:284
  15.8 0.0 copy-done.1
  15.8 0.1 copy.7
  15.9 0.1 reshape.15
  16.0 0.1 pad_add_fusion.2
  16.1 0.3 collective-permute-start
  16.3 6.3 %collective-permute-done = s32[1,9]{1,0:T(1,128)S(1)} collective-permute-done((s32[1,9]{1,0:T(1,128)S(1)}, s32[1,9]{1,0:T(1,128)S(1)}, u32[]{:S(2)}, u32[]{:S(2)}) %collective-permute-start) | collective-permute-done | bytes 68 | tf_op jit(solution)/shard_map/ppermute | solution.py:200
  22.7 0.2 collective-permute-start.1
  22.9 2.5 %collective-permute-done.1 = s32[2,9]{1,0:T(2,128)S(1)} collective-permute-done((s32[2,9]{1,0:T(2,128)S(1)}, s32[2,9]{1,0:T(2,128)S(1)}, u32[]{:S(2)}, u32[]{:S(2)}) %collective-permute-start.1) | collective-permute-done | bytes 104 | tf_op jit(solution)/shard_map/ppermute | solution.py:200
  25.5 1.2 %collective-permute-start.2 = (s32[4,9]{1,0:T(4,128)S(1)}, s32[4,9]{1,0:T(4,128)S(1)}, u32[]{:S(2)}, u32[]{:S(2)}) collective-permute-start(s32[4,9]{1,0:T(4,128)S(1)} %pad_add_fusion), channel_id=1, source_target_pairs={{0,16},{4,20},{8,24},{12,28},{16,0},{20,4},{24,8},{28,12},{1,17},{... | collective-permute-start | bytes 440 | tf_op jit(solution)/shard_map/ppermute | solution.py:200
  26.7 1.6 %collective-permute-done.2 = s32[4,9]{1,0:T(4,128)S(1)} collective-permute-done((s32[4,9]{1,0:T(4,128)S(1)}, s32[4,9]{1,0:T(4,128)S(1)}, u32[]{:S(2)}, u32[]{:S(2)}) %collective-permute-start.2) | collective-permute-done | bytes 176 | tf_op jit(solution)/shard_map/ppermute | solution.py:200
  28.3 13.2 %all-to-all-done.w = bf16[32,8,2048]{2,1,0:T(8,128)(2,1)S(1)} async-done(((bf16[32,8,2048]{2,1,0:T(8,128)(2,1)}), bf16[32,8,2048]{2,1,0:T(8,128)(2,1)S(1)}, u32[]{:S(2)}, u32[]{:S(2)}) %all-to-all-start) | async-done | bytes 1048608 | tf_op jit(solution)/shard_map/all_to_all | solution.py:284
  41.5 2.7 %cross.1 = bf16[256,1024]{1,0:T(8,128)(2,1)S(1)} custom-call(s32[8,9]{1,0:T(8,128)S(1)} %constant_dynamic-slice_fusion.info, bf16[32,8,2048]{2,1,0:T(8,128)(2,1)S(1)} %all-to-all-done.w), custom_call_target="tpu_custom_call" | custom-call | flops 16777216 | bytes 1572864 | tf_op jit(solution)/shard_map/cross/pallas_call | solution.py:162
  44.2 18.3 %all_to_all.10 = bf16[32,8,1024]{2,1,0:T(8,128)(2,1)S(1)} all-to-all(bf16[32,8,1024]{2,1,0:T(8,128)(2,1)S(1)} %bitcast.5), channel_id=1, replica_groups=mesh['chan'=8,'tm'=4] {'chan','tm'}, dimensions={0} | all-to-all | bytes 1048576 | tf_op jit(solution)/shard_map/all_to_all | solution.py:293
  62.5 0.0 copy-done
  62.5 2.6 %inverse.1 = f32[128,2048]{1,0:T(8,128)} custom-call(bf16[256,1024]{1,0:T(8,128)(2,1)S(1)} %bitcast.6, f32[128,1024]{1,0:T(8,128)S(1)} %copy-done), custom_call_target="tpu_custom_call" | custom-call | flops 1073741824 | bytes 1572864 | tf_op jit(solution)/shard_map/inverse/pallas_call | solution.py:246
  (4 shorter events, 0.1 us)
Async XLA Ops:
  8.0 7.8 %copy-start.1 = (s32[4,2]{0,1:T(2,128)S(1)}, s32[4,2]{0,1:T(2,128)}, u32[]{:S(2)}) copy-start(s32[4,2]{0,1:T(2,128)} %param.6) | copy-start | bytes 100
  8.0 54.5 %copy-start = (f32[128,1024]{1,0:T(8,128)S(1)}, f32[128,1024]{1,0:T(8,128)}, u32[]{:S(2)}) copy-start(f32[128,1024]{1,0:T(8,128)} %constant.33.clone.seeds) | copy-start | bytes 1572868
  8.0 33.5 %all-to-all-start = ((bf16[32,8,2048]{2,1,0:T(8,128)(2,1)}), bf16[32,8,2048]{2,1,0:T(8,128)(2,1)S(1)}, u32[]{:S(2)}, u32[]{:S(2)}) async-start(bf16[32,8,2048]{2,1,0:T(8,128)(2,1)} %bitcast.1), calls=%async_computation | async-start | bytes 2097152 | tf_op jit(solution)/shard_map/all_to_all | solution.py:284
  16.1 6.6 %collective-permute-start = (s32[1,9]{1,0:T(1,128)S(1)}, s32[1,9]{1,0:T(1,128)S(1)}, u32[]{:S(2)}, u32[]{:S(2)}) collective-permute-start(s32[1,9]{1,0:T(1,128)S(1)} %pad_add_fusion.2), channel_id=1, source_target_pairs={{0,28},{4,0},{8,4},{12,8},{16,12},{20,16},{24,20},{28,24},{1,29},{... | collective-permute-start | bytes 116 | tf_op jit(solution)/shard_map/ppermute | solution.py:200
  22.7 2.8 %collective-permute-start.1 = (s32[2,9]{1,0:T(2,128)S(1)}, s32[2,9]{1,0:T(2,128)S(1)}, u32[]{:S(2)}, u32[]{:S(2)}) collective-permute-start(s32[2,9]{1,0:T(2,128)S(1)} %pad_add_fusion.1), channel_id=1, source_target_pairs={{0,24},{4,28},{8,0},{12,4},{16,8},{20,12},{24,16},{28,20},{1,25},{... | collective-permute-start | bytes 224 | tf_op jit(solution)/shard_map/ppermute | solution.py:200
  25.5 2.8 %collective-permute-start.2 = (s32[4,9]{1,0:T(4,128)S(1)}, s32[4,9]{1,0:T(4,128)S(1)}, u32[]{:S(2)}, u32[]{:S(2)}) collective-permute-start(s32[4,9]{1,0:T(4,128)S(1)} %pad_add_fusion), channel_id=1, source_target_pairs={{0,16},{4,20},{8,24},{12,28},{16,0},{20,4},{24,8},{28,12},{1,17},{... | collective-permute-start | bytes 440 | tf_op jit(solution)/shard_map/ppermute | solution.py:200

commit v2 on v1

--- a/solution.py
+++ b/solution.py
@@ -19,7 +19,7 @@
 QUARTER = NS // TURN
 GROUP = FB // TURN
 STEP = 32
-VMEM = 24 * 1024 * 1024
+VMEM = 28 * 1024 * 1024
 
 
 def bins():
@@ -34,7 +34,7 @@
 def forward_seeds():
     coarse = wave(STEP * np.arange(QUARTER // STEP), bins())
     fine = wave(np.arange(STEP), bins())
-    return np.concatenate(coarse + fine)
+    return np.concatenate(coarse + fine).reshape(-1, TURN, GROUP).swapaxes(0, 1).copy()
 
 
 def inverse_seeds():
@@ -44,44 +44,82 @@
     return np.concatenate(coarse + fine)
 
 
-def forward_kernel(x_hbm, seeds_hbm, out, x, seeds, spec, table, plus, minus, sems):
-    rows = spec.shape[0]
-    seed_copy = pltpu.make_async_copy(seeds_hbm, seeds, sems.at[0])
-    x_copy = pltpu.make_async_copy(x_hbm, x, sems.at[1])
-    seed_copy.start()
-    x_copy.start()
-    seed_copy.wait()
+def forward_kernel(x_hbm, seeds_hbm, out_hbm, x, seeds, table, left, spec, out, seed_sem, x_sem, out_sem):
+    rows, parts = spec.shape[0], x_sem.shape[0]
+    channels = x.shape[0] // parts
+    seed_copies = [pltpu.make_async_copy(seeds_hbm.at[g], seeds.at[g], seed_sem.at[g]) for g in range(TURN)]
+    x_copies = []
+    for k in range(parts):
+        at = pl.ds(k * channels, channels)
+        x_copies.append(pltpu.make_async_copy(x_hbm.at[at], x.at[at], x_sem.at[k]))
+    for copy in seed_copies + x_copies:
+        copy.start()
     coarse = QUARTER // STEP
+
+    def fill(g):
+        seed_copies[g].wait()
+        fc, fs = seeds[g, 2 * coarse : 2 * coarse + STEP, :], seeds[g, 2 * coarse + STEP :, :]
+        for i in range(coarse):
+            c, s = seeds[g, i : i + 1, :], seeds[g, coarse + i : coarse + i + 1, :]
+            at = slice(i * STEP, (i + 1) * STEP)
+            table[g, at, :GROUP] = (c * fc - s * fs).astype(jnp.bfloat16)
+            table[g, at, GROUP:] = -(s * fc + c * fs).astype(jnp.bfloat16)
+
+    early = 4
+    for g in range(early):
+        fill(g)
+    for copy in x_copies:
+        copy.wait()
+    lanes = 256
+    for offset in range(0, QUARTER, lanes):
+        into = slice(offset, offset + lanes)
+        quarters = []
+        for m in range(TURN):
+            quarter = x[:, :, m * QUARTER + offset : m * QUARTER + offset + lanes].reshape(rows, lanes)
+            left[m, :, into] = quarter
+            left[TURN + m, :, into] = -quarter
+            quarters.append(quarter.astype(jnp.float32))
+        even, odd = quarters[0] + quarters[2], quarters[1] + quarters[3]
+        for k, value in enumerate((even + odd, even - odd)):
+            high = value.astype(jnp.bfloat16)
+            left[2 * TURN + 2 * k, :, into] = high
+            left[2 * TURN + 2 * k + 1, :, into] = (value - high.astype(jnp.float32)).astype(jnp.bfloat16)
+    power = jnp.zeros((rows, GROUP), jnp.float32)
     for g in range(TURN):
-        columns = slice(g * GROUP, (g + 1) * GROUP)
-        cosine, sine = table.at[g % 2, :, :GROUP], table.at[g % 2, :, GROUP:]
-        for i in range(coarse):
-            c, s = seeds[i : i + 1, columns], seeds[coarse + i : coarse + i + 1, columns]
-            fc, fs = seeds[2 * coarse : 2 * coarse + STEP, columns], seeds[2 * coarse + STEP :, columns]
-            at = slice(i * STEP, (i + 1) * STEP)
-            cosine[at, :] = (c * fc - s * fs).astype(jnp.bfloat16)
-            sine[at, :] = -(s * fc + c * fs).astype(jnp.bfloat16)
-        if g == 0:
-            x_copy.wait()
-            for m in range(TURN):
-                samples = slice(m * QUARTER, (m + 1) * QUARTER)
-                quarter = x[:, :, samples].reshape(rows, QUARTER)
-                plus[:, samples] = quarter
-                minus[:, samples] = -quarter
-        phases = [(F_LO + g) * m % 4 for m in range(TURN)]
-        real = [[(1, cosine), (1, sine), (-1, cosine), (-1, sine)][p] for p in phases]
-        imag = [[(1, sine), (-1, cosine), (-1, sine), (1, cosine)][p] for p in phases]
-        for start, terms in ((0, real), (FB, imag)):
-            left = [
-                (plus if sign > 0 else minus)[:, m * QUARTER : (m + 1) * QUARTER] for m, (sign, _) in enumerate(terms)
-            ]
-            right = [half[...] for _, half in terms]
-            spec[:, start + g * GROUP : start + (g + 1) * GROUP] = jnp.dot(
-                jnp.concatenate(left, axis=1), jnp.concatenate(right, axis=0), preferred_element_type=jnp.float32
+        if g >= early:
+            fill(g)
+        cosine, sine = table[g, :, :GROUP], table[g, :, GROUP:]
+        turn = (F_LO + g) % TURN
+        if turn % 2 == 0:
+            pair = jnp.concatenate([left[2 * TURN + turn], left[2 * TURN + turn + 1]], axis=1)
+            real = jnp.dot(pair, jnp.concatenate([cosine] * 2, axis=0), preferred_element_type=jnp.float32)
+            imag = jnp.dot(pair, jnp.concatenate([sine] * 2, axis=0), preferred_element_type=jnp.float32)
+        else:
+            ahead = (0, 1, TURN + 2, TURN + 3) if turn == 1 else (0, TURN + 1, TURN + 2, 3)
+            behind = (0, TURN + 1, TURN + 2, 3) if turn == 1 else (0, 1, TURN + 2, TURN + 3)
+            real = jnp.dot(
+                jnp.concatenate([left[k] for k in ahead], axis=1),
+                jnp.concatenate([cosine, sine] * 2, axis=0),
+                preferred_element_type=jnp.float32,
             )
-    spectrum = spec[...]
-    mean_power = jnp.sum(spectrum * spectrum, axis=1, keepdims=True) / FB
-    out[...] = (spectrum * lax.rsqrt(mean_power + 1e-06)).astype(jnp.bfloat16)
+            imag = jnp.dot(
+                jnp.concatenate([left[k] for k in behind], axis=1),
+                jnp.concatenate([sine, cosine] * 2, axis=0),
+                preferred_element_type=jnp.float32,
+            )
+        spec[:, g * GROUP : (g + 1) * GROUP] = real
+        spec[:, FB + g * GROUP : FB + (g + 1) * GROUP] = imag
+        power = power + real * real + imag * imag
+    scale = lax.rsqrt(jnp.sum(power, axis=1, keepdims=True) / FB + 1e-06)
+    out_copies = []
+    pieces = out_sem.shape[0]
+    for k in range(pieces):
+        at = slice(k * rows // pieces, (k + 1) * rows // pieces)
+        out[at, :] = (spec[at, :] * scale[at, :]).astype(jnp.bfloat16)
+        out_copies.append(pltpu.make_async_copy(out.at[at], out_hbm.at[at], out_sem.at[k]))
+        out_copies[-1].start()
+    for copy in out_copies:
+        copy.wait()
 
 
 def in_hbm(array):
@@ -95,15 +133,17 @@
         forward_kernel,
         out_shape=jax.ShapeDtypeStruct((rows, 2 * FB), jnp.bfloat16),
         in_specs=[pl.BlockSpec(memory_space=pltpu.HBM)] * 2,
-        out_specs=pl.BlockSpec(memory_space=pltpu.VMEM),
+        out_specs=pl.BlockSpec(memory_space=pltpu.HBM),
         scratch_shapes=[
             pltpu.VMEM(traces.shape, jnp.bfloat16),
             pltpu.VMEM(seeds.shape, jnp.float32),
+            pltpu.VMEM((TURN, QUARTER, 2 * GROUP), jnp.bfloat16),
+            pltpu.VMEM((3 * TURN, rows, QUARTER), jnp.bfloat16),
             pltpu.VMEM((rows, 2 * FB), jnp.float32),
-            pltpu.VMEM((2, QUARTER, 2 * GROUP), jnp.bfloat16),
-            pltpu.VMEM((rows, NS), jnp.bfloat16),
-            pltpu.VMEM((rows, NS), jnp.bfloat16),
-            pltpu.SemaphoreType.DMA((2,)),
+            pltpu.VMEM((rows, 2 * FB), jnp.bfloat16),
+            pltpu.SemaphoreType.DMA((TURN,)),
+            pltpu.SemaphoreType.DMA((4,)),
+            pltpu.SemaphoreType.DMA((4,)),
         ],
         compiler_params=pltpu.CompilerParams(vmem_limit_bytes=VMEM),
         cost_estimate=pl.CostEstimate(
@@ -209,18 +249,17 @@
     lanes = 256
     target = lax.broadcasted_iota(jnp.int32, (rows, rows), 0)
     source = lax.broadcasted_iota(jnp.int32, (rows, rows), 1)
-    channel, part = source // 8 * 4 + source % 4, source // 4 % 2
-    first = (target < rows // 2) & (target == channel)
-    second = target == channel + rows // 2
+    wanted = source // 8 * 4 + source % 4 + source // 4 % 2 * (rows // 2)
+    pick = jnp.where(target == wanted, 1.0, 0.0).astype(jnp.bfloat16)
     for g in range(TURN):
         columns = slice(g * GROUP, (g + 1) * GROUP)
-        sign, swap = [(1, 0), (-1, 1), (-1, 0), (1, 1)][(F_LO + g) % 4]
-        for meets in range(2):
-            turned = (-sign if swap and meets else sign) * jnp.where(part == (meets ^ swap), 1.0, 0.0)
-            pick = jnp.where(first, jnp.where(part == meets, 1.0, 0.0), jnp.where(second, turned, 0.0))
-            ordered[:, meets * FB + g * GROUP : meets * FB + (g + 1) * GROUP] = jnp.dot(
-                pick.astype(jnp.bfloat16), y[:, columns], preferred_element_type=jnp.float32
-            ).astype(jnp.bfloat16)
+        moved = jnp.dot(pick, y[:, columns], preferred_element_type=jnp.float32)
+        real, imag = moved[: rows // 2], moved[rows // 2 :]
+        far = [(real, imag), (-imag, real), (-real, -imag), (imag, -real)][(F_LO + g) % TURN]
+        for k, (near_side, far_side) in enumerate(zip((real, imag), far)):
+            into = slice(k * FB + g * GROUP, k * FB + (g + 1) * GROUP)
+            ordered[: rows // 2, into] = near_side.astype(jnp.bfloat16)
+            ordered[rows // 2 :, into] = far_side.astype(jnp.bfloat16)
     copies = []
     for k, offset in enumerate(range(0, half, lanes)):
         columns = slice(offset, offset + lanes)

time: 65.3 us -> 64.7 us (level)
  no operation moved by 1% of the time
where the time goes in v2:
time: 64.7 us
  waiting for transfers between devices  23.6 us (36%)
  blocking collectives  18.3 us (28%)
  Pallas kernels  12.9 us (20%)
  starting transfers between devices  8.86 us (14%)
  between operations  0.71 us (1%)
    all_to_all x1, blocking collectives, on_device(): own = lax.all_to_all(cross, AXES, split_axis=0, concat_axis=0, tiled=True)  18.3 us
    all_to_all x1, waiting for transfers between devices, on_device(): lax.all_to_all(sent, AXES, split_axis=0, concat_axis=0, tiled=True)  13.2 us
    ppermute x3, waiting for transfers between devices, every_owner(): lax.ppermute(ring, 'chan', [(source, (source - hop) % owners) for source...  10.4 us
    pallas_call x1, Pallas kernels, forward(): pl.pallas_call(forward_kernel, out_shape=jax.ShapeDtypeStruct((rows, 2 *...  7.68 us
    all_to_all x1, starting transfers between devices, on_device(): lax.all_to_all(sent, AXES, split_axis=0, concat_axis=0, tiled=True)  7.1 us
    pallas_call x1, Pallas kernels, cross_fast(): pl.pallas_call(functools.partial(cross_kernel, slots, groups), out_shape=...  2.88 us
    pallas_call x1, Pallas kernels, inverse(): pl.pallas_call(functools.partial(inverse_kernel, scale), out_shape=jax.Sh...  2.35 us
    ppermute x3, starting transfers between devices, every_owner(): lax.ppermute(ring, 'chan', [(source, (source - hop) % owners) for source...  1.76 us
  transfers between devices with their start and end apart: 4, of which 4 were waited for; matrix products, arithmetic and copies ran while one was open for 0% of the time, Pallas kernels for 0%

profile of v2, /device:TPU:1, one launch (start us, length us, event | category | flops | bytes accessed | tf_op | source)
XLA Modules:
  0.0 64.7 jit_solution(11158547008440356488)
XLA Ops:
  0.0 7.7 %forward.1 = bf16[256,2048]{1,0:T(8,128)(2,1)} custom-call(bf16[128,2,4096]{2,1,0:T(2,128)(2,1)} %x_hbm.1, f32[4,128,256]{2,1,0:T(8,128)} %constant.32.clone.seeds_hbm), custom_call_target="tpu_custom_call" | custom-call | flops 4294967296 | bytes 3145728 | tf_op jit(solution)/shard_map/forward/pallas_call | solution.py:132
  7.7 0.0 copy-start.1
  7.7 0.0 copy-start
  7.7 7.1 %all-to-all-start = ((bf16[32,8,2048]{2,1,0:T(8,128)(2,1)}), bf16[32,8,2048]{2,1,0:T(8,128)(2,1)S(1)}, u32[]{:S(2)}, u32[]{:S(2)}) async-start(bf16[32,8,2048]{2,1,0:T(8,128)(2,1)} %bitcast.1), calls=%async_computation | async-start | bytes 2097152 | tf_op jit(solution)/shard_map/all_to_all | solution.py:323
  15.5 0.0 copy-done.1
  15.5 0.1 copy.7
  15.6 0.1 reshape.15
  15.7 0.1 pad_add_fusion.2
  15.7 0.3 collective-permute-start
  16.0 6.3 %collective-permute-done = s32[1,9]{1,0:T(1,128)S(1)} collective-permute-done((s32[1,9]{1,0:T(1,128)S(1)}, s32[1,9]{1,0:T(1,128)S(1)}, u32[]{:S(2)}, u32[]{:S(2)}) %collective-permute-start) | collective-permute-done | bytes 68 | tf_op jit(solution)/shard_map/ppermute | solution.py:240
  22.4 0.2 collective-permute-start.1
  22.6 2.5 %collective-permute-done.1 = s32[2,9]{1,0:T(2,128)S(1)} collective-permute-done((s32[2,9]{1,0:T(2,128)S(1)}, s32[2,9]{1,0:T(2,128)S(1)}, u32[]{:S(2)}, u32[]{:S(2)}) %collective-permute-start.1) | collective-permute-done | bytes 104 | tf_op jit(solution)/shard_map/ppermute | solution.py:240
  25.1 1.2 %collective-permute-start.2 = (s32[4,9]{1,0:T(4,128)S(1)}, s32[4,9]{1,0:T(4,128)S(1)}, u32[]{:S(2)}, u32[]{:S(2)}) collective-permute-start(s32[4,9]{1,0:T(4,128)S(1)} %pad_add_fusion), channel_id=1, source_target_pairs={{0,16},{4,20},{8,24},{12,28},{16,0},{20,4},{24,8},{28,12},{1,17},{... | collective-permute-start | bytes 440 | tf_op jit(solution)/shard_map/ppermute | solution.py:240
  26.4 1.6 %collective-permute-done.2 = s32[4,9]{1,0:T(4,128)S(1)} collective-permute-done((s32[4,9]{1,0:T(4,128)S(1)}, s32[4,9]{1,0:T(4,128)S(1)}, u32[]{:S(2)}, u32[]{:S(2)}) %collective-permute-start.2) | collective-permute-done | bytes 176 | tf_op jit(solution)/shard_map/ppermute | solution.py:240
  28.0 13.2 %all-to-all-done.w = bf16[32,8,2048]{2,1,0:T(8,128)(2,1)S(1)} async-done(((bf16[32,8,2048]{2,1,0:T(8,128)(2,1)}), bf16[32,8,2048]{2,1,0:T(8,128)(2,1)S(1)}, u32[]{:S(2)}, u32[]{:S(2)}) %all-to-all-start) | async-done | bytes 1048608 | tf_op jit(solution)/shard_map/all_to_all | solution.py:323
  41.2 2.9 %cross.1 = bf16[256,1024]{1,0:T(8,128)(2,1)S(1)} custom-call(s32[8,9]{1,0:T(8,128)S(1)} %constant_dynamic-slice_fusion.info, bf16[32,8,2048]{2,1,0:T(8,128)(2,1)S(1)} %all-to-all-done.w), custom_call_target="tpu_custom_call" | custom-call | flops 16777216 | bytes 1572864 | tf_op jit(solution)/shard_map/cross/pallas_call | solution.py:202
  44.1 18.3 %all_to_all.10 = bf16[32,8,1024]{2,1,0:T(8,128)(2,1)S(1)} all-to-all(bf16[32,8,1024]{2,1,0:T(8,128)(2,1)S(1)} %bitcast.5), channel_id=1, replica_groups=mesh['chan'=8,'tm'=4] {'chan','tm'}, dimensions={0} | all-to-all | bytes 1048576 | tf_op jit(solution)/shard_map/all_to_all | solution.py:332
  62.3 0.0 copy-done
  62.3 2.3 %inverse.1 = f32[128,2048]{1,0:T(8,128)} custom-call(bf16[256,1024]{1,0:T(8,128)(2,1)S(1)} %bitcast.6, f32[128,1024]{1,0:T(8,128)S(1)} %copy-done), custom_call_target="tpu_custom_call" | custom-call | flops 1073741824 | bytes 1572864 | tf_op jit(solution)/shard_map/inverse/pallas_call | solution.py:285
  (4 shorter events, 0.1 us)
Async XLA Ops:
  7.7 7.8 %copy-start.1 = (s32[4,2]{0,1:T(2,128)S(1)}, s32[4,2]{0,1:T(2,128)}, u32[]{:S(2)}) copy-start(s32[4,2]{0,1:T(2,128)} %param.6) | copy-start | bytes 100
  7.7 54.6 %copy-start = (f32[128,1024]{1,0:T(8,128)S(1)}, f32[128,1024]{1,0:T(8,128)}, u32[]{:S(2)}) copy-start(f32[128,1024]{1,0:T(8,128)} %constant.33.clone.seeds) | copy-start | bytes 1572868
  7.7 33.5 %all-to-all-start = ((bf16[32,8,2048]{2,1,0:T(8,128)(2,1)}), bf16[32,8,2048]{2,1,0:T(8,128)(2,1)S(1)}, u32[]{:S(2)}, u32[]{:S(2)}) async-start(bf16[32,8,2048]{2,1,0:T(8,128)(2,1)} %bitcast.1), calls=%async_computation | async-start | bytes 2097152 | tf_op jit(solution)/shard_map/all_to_all | solution.py:323
  15.7 6.6 %collective-permute-start = (s32[1,9]{1,0:T(1,128)S(1)}, s32[1,9]{1,0:T(1,128)S(1)}, u32[]{:S(2)}, u32[]{:S(2)}) collective-permute-start(s32[1,9]{1,0:T(1,128)S(1)} %pad_add_fusion.2), channel_id=1, source_target_pairs={{0,28},{4,0},{8,4},{12,8},{16,12},{20,16},{24,20},{28,24},{1,29},{... | collective-permute-start | bytes 116 | tf_op jit(solution)/shard_map/ppermute | solution.py:240
  22.4 2.8 %collective-permute-start.1 = (s32[2,9]{1,0:T(2,128)S(1)}, s32[2,9]{1,0:T(2,128)S(1)}, u32[]{:S(2)}, u32[]{:S(2)}) collective-permute-start(s32[2,9]{1,0:T(2,128)S(1)} %pad_add_fusion.1), channel_id=1, source_target_pairs={{0,24},{4,28},{8,0},{12,4},{16,8},{20,12},{24,16},{28,20},{1,25},{... | collective-permute-start | bytes 224 | tf_op jit(solution)/shard_map/ppermute | solution.py:240
  25.1 2.8 %collective-permute-start.2 = (s32[4,9]{1,0:T(4,128)S(1)}, s32[4,9]{1,0:T(4,128)S(1)}, u32[]{:S(2)}, u32[]{:S(2)}) collective-permute-start(s32[4,9]{1,0:T(4,128)S(1)} %pad_add_fusion), channel_id=1, source_target_pairs={{0,16},{4,20},{8,24},{12,28},{16,0},{20,4},{24,8},{28,12},{1,17},{... | collective-permute-start | bytes 440 | tf_op jit(solution)/shard_map/ppermute | solution.py:240

commit v3 on v2

--- a/solution.py
+++ b/solution.py
@@ -52,7 +52,7 @@
     for k in range(parts):
         at = pl.ds(k * channels, channels)
         x_copies.append(pltpu.make_async_copy(x_hbm.at[at], x.at[at], x_sem.at[k]))
-    for copy in seed_copies + x_copies:
+    for copy in seed_copies[1:2] + x_copies[:1] + seed_copies[3:] + x_copies[1:2] + seed_copies[:1] + x_copies[2:3] + seed_copies[2:3] + x_copies[3:]:
         copy.start()
     coarse = QUARTER // STEP
 
@@ -65,29 +65,34 @@
             table[g, at, :GROUP] = (c * fc - s * fs).astype(jnp.bfloat16)
             table[g, at, GROUP:] = -(s * fc + c * fs).astype(jnp.bfloat16)
 
-    early = 4
-    for g in range(early):
+    for g in (1, 3, 0, 2):
         fill(g)
-    for copy in x_copies:
+    lanes = QUARTER
+    for k, copy in enumerate(x_copies):
         copy.wait()
-    lanes = 256
-    for offset in range(0, QUARTER, lanes):
-        into = slice(offset, offset + lanes)
-        quarters = []
+        here = slice(k * rows // parts, (k + 1) * rows // parts)
         for m in range(TURN):
-            quarter = x[:, :, m * QUARTER + offset : m * QUARTER + offset + lanes].reshape(rows, lanes)
-            left[m, :, into] = quarter
-            left[TURN + m, :, into] = -quarter
-            quarters.append(quarter.astype(jnp.float32))
-        even, odd = quarters[0] + quarters[2], quarters[1] + quarters[3]
-        for k, value in enumerate((even + odd, even - odd)):
-            high = value.astype(jnp.bfloat16)
-            left[2 * TURN + 2 * k, :, into] = high
-            left[2 * TURN + 2 * k + 1, :, into] = (value - high.astype(jnp.float32)).astype(jnp.bfloat16)
+            quarter = x[k * channels : (k + 1) * channels, :, m * QUARTER : (m + 1) * QUARTER].reshape(rows // parts, QUARTER)
+            left[m, here, :] = quarter
+            if m:
+                left[TURN + m, here, :] = -quarter
+
+    def add_quarters():
+        for offset in range(0, QUARTER, lanes):
+            into = slice(offset, offset + lanes)
+            quarters = [left[m, :, into].astype(jnp.float32) for m in range(TURN)]
+            even, odd = quarters[0] + quarters[2], quarters[1] + quarters[3]
+            for k, value in enumerate((even + odd, even - odd)):
+                high = value.astype(jnp.bfloat16)
+                left[2 * TURN + 2 * k, :, into] = high
+                left[2 * TURN + 2 * k + 1, :, into] = (value - high.astype(jnp.float32)).astype(jnp.bfloat16)
+
     power = jnp.zeros((rows, GROUP), jnp.float32)
-    for g in range(TURN):
-        if g >= early:
+    for at_g, g in enumerate((1, 3, 0, 2)):
+        if g not in (1, 3, 0, 2):
             fill(g)
+        if at_g == 2:
+            add_quarters()
         cosine, sine = table[g, :, :GROUP], table[g, :, GROUP:]
         turn = (F_LO + g) % TURN
         if turn % 2 == 0:

time: 64.7 us -> 64.3 us (level)
  transfers between devices with their start and end apart: 4 -> 4, of which waited for: 4 -> 4; matrix products, arithmetic and copies ran while one was open for 0% -> 1% of each run, Pallas kernels for 0% -> 0%
where the time goes in v3:
time: 64.3 us; the launch traced here: 64.2 us
  waiting for transfers between devices  23.6 us (37%)
  blocking collectives  18.3 us (28%)
  Pallas kernels  12.4 us (19%)
  starting transfers between devices  8.86 us (14%)
  between operations  0.71 us (1%)
    all_to_all x1, blocking collectives, on_device(): own = lax.all_to_all(cross, AXES, split_axis=0, concat_axis=0, tiled=True)  18.3 us
    all_to_all x1, waiting for transfers between devices, on_device(): lax.all_to_all(sent, AXES, split_axis=0, concat_axis=0, tiled=True)  13.2 us
    ppermute x3, waiting for transfers between devices, every_owner(): lax.ppermute(ring, 'chan', [(source, (source - hop) % owners) for source...  10.4 us
    all_to_all x1, starting transfers between devices, on_device(): lax.all_to_all(sent, AXES, split_axis=0, concat_axis=0, tiled=True)  7.11 us
    pallas_call x1, Pallas kernels, forward(): pl.pallas_call(forward_kernel, out_shape=jax.ShapeDtypeStruct((rows, 2 *...  7.08 us
    pallas_call x1, Pallas kernels, cross_fast(): pl.pallas_call(functools.partial(cross_kernel, slots, groups), out_shape=...  2.99 us
    pallas_call x1, Pallas kernels, inverse(): pl.pallas_call(functools.partial(inverse_kernel, scale), out_shape=jax.Sh...  2.35 us
    ppermute x3, starting transfers between devices, every_owner(): lax.ppermute(ring, 'chan', [(source, (source - hop) % owners) for source...  1.76 us
  transfers between devices with their start and end apart: 4, of which 4 were waited for; matrix products, arithmetic and copies ran while one was open for 1% of the time, Pallas kernels for 0%

profile of v3, /device:TPU:1, one launch (start us, length us, event | category | flops | bytes accessed | tf_op | source)
XLA Modules:
  0.0 64.2 jit_solution(10681512371841171806)
XLA Ops:
  0.0 7.1 %forward.1 = bf16[256,2048]{1,0:T(8,128)(2,1)} custom-call(bf16[128,2,4096]{2,1,0:T(2,128)(2,1)} %x_hbm.1, f32[4,128,256]{2,1,0:T(8,128)} %constant.32.clone.seeds_hbm), custom_call_target="tpu_custom_call" | custom-call | flops 4294967296 | bytes 3145728 | tf_op jit(solution)/shard_map/forward/pallas_call | solution.py:137
  7.1 0.0 copy-start.1
  7.1 0.0 copy-start
  7.1 7.1 %all-to-all-start = ((bf16[32,8,2048]{2,1,0:T(8,128)(2,1)}), bf16[32,8,2048]{2,1,0:T(8,128)(2,1)S(1)}, u32[]{:S(2)}, u32[]{:S(2)}) async-start(bf16[32,8,2048]{2,1,0:T(8,128)(2,1)} %bitcast.1), calls=%async_computation | async-start | bytes 2097152 | tf_op jit(solution)/shard_map/all_to_all | solution.py:328
  14.9 0.0 copy-done.1
  14.9 0.1 copy.7
  15.0 0.1 reshape.15
  15.1 0.1 pad_add_fusion.2
  15.1 0.3 collective-permute-start
  15.4 6.3 %collective-permute-done = s32[1,9]{1,0:T(1,128)S(1)} collective-permute-done((s32[1,9]{1,0:T(1,128)S(1)}, s32[1,9]{1,0:T(1,128)S(1)}, u32[]{:S(2)}, u32[]{:S(2)}) %collective-permute-start) | collective-permute-done | bytes 68 | tf_op jit(solution)/shard_map/ppermute | solution.py:245
  21.8 0.2 collective-permute-start.1
  22.0 2.5 %collective-permute-done.1 = s32[2,9]{1,0:T(2,128)S(1)} collective-permute-done((s32[2,9]{1,0:T(2,128)S(1)}, s32[2,9]{1,0:T(2,128)S(1)}, u32[]{:S(2)}, u32[]{:S(2)}) %collective-permute-start.1) | collective-permute-done | bytes 104 | tf_op jit(solution)/shard_map/ppermute | solution.py:245
  24.5 1.2 %collective-permute-start.2 = (s32[4,9]{1,0:T(4,128)S(1)}, s32[4,9]{1,0:T(4,128)S(1)}, u32[]{:S(2)}, u32[]{:S(2)}) collective-permute-start(s32[4,9]{1,0:T(4,128)S(1)} %pad_add_fusion), channel_id=1, source_target_pairs={{0,16},{4,20},{8,24},{12,28},{16,0},{20,4},{24,8},{28,12},{1,17},{... | collective-permute-start | bytes 440 | tf_op jit(solution)/shard_map/ppermute | solution.py:245
  25.8 1.6 %collective-permute-done.2 = s32[4,9]{1,0:T(4,128)S(1)} collective-permute-done((s32[4,9]{1,0:T(4,128)S(1)}, s32[4,9]{1,0:T(4,128)S(1)}, u32[]{:S(2)}, u32[]{:S(2)}) %collective-permute-start.2) | collective-permute-done | bytes 176 | tf_op jit(solution)/shard_map/ppermute | solution.py:245
  27.4 13.2 %all-to-all-done.w = bf16[32,8,2048]{2,1,0:T(8,128)(2,1)S(1)} async-done(((bf16[32,8,2048]{2,1,0:T(8,128)(2,1)}), bf16[32,8,2048]{2,1,0:T(8,128)(2,1)S(1)}, u32[]{:S(2)}, u32[]{:S(2)}) %all-to-all-start) | async-done | bytes 1048608 | tf_op jit(solution)/shard_map/all_to_all | solution.py:328
  40.6 3.0 %cross.1 = bf16[256,1024]{1,0:T(8,128)(2,1)S(1)} custom-call(s32[8,9]{1,0:T(8,128)S(1)} %constant_dynamic-slice_fusion.info, bf16[32,8,2048]{2,1,0:T(8,128)(2,1)S(1)} %all-to-all-done.w), custom_call_target="tpu_custom_call" | custom-call | flops 16777216 | bytes 1572864 | tf_op jit(solution)/shard_map/cross/pallas_call | solution.py:207
  43.6 18.3 %all_to_all.10 = bf16[32,8,1024]{2,1,0:T(8,128)(2,1)S(1)} all-to-all(bf16[32,8,1024]{2,1,0:T(8,128)(2,1)S(1)} %bitcast.5), channel_id=1, replica_groups=mesh['chan'=8,'tm'=4] {'chan','tm'}, dimensions={0} | all-to-all | bytes 1048576 | tf_op jit(solution)/shard_map/all_to_all | solution.py:337
  61.8 0.0 copy-done
  61.8 2.4 %inverse.1 = f32[128,2048]{1,0:T(8,128)} custom-call(bf16[256,1024]{1,0:T(8,128)(2,1)S(1)} %bitcast.6, f32[128,1024]{1,0:T(8,128)S(1)} %copy-done), custom_call_target="tpu_custom_call" | custom-call | flops 1073741824 | bytes 1572864 | tf_op jit(solution)/shard_map/inverse/pallas_call | solution.py:290
  (4 shorter events, 0.1 us)
Async XLA Ops:
  7.1 7.8 %copy-start.1 = (s32[4,2]{0,1:T(2,128)S(1)}, s32[4,2]{0,1:T(2,128)}, u32[]{:S(2)}) copy-start(s32[4,2]{0,1:T(2,128)} %param.6) | copy-start | bytes 100
  7.1 54.7 %copy-start = (f32[128,1024]{1,0:T(8,128)S(1)}, f32[128,1024]{1,0:T(8,128)}, u32[]{:S(2)}) copy-start(f32[128,1024]{1,0:T(8,128)} %constant.33.clone.seeds) | copy-start | bytes 1572868
  7.1 33.5 %all-to-all-start = ((bf16[32,8,2048]{2,1,0:T(8,128)(2,1)}), bf16[32,8,2048]{2,1,0:T(8,128)(2,1)S(1)}, u32[]{:S(2)}, u32[]{:S(2)}) async-start(bf16[32,8,2048]{2,1,0:T(8,128)(2,1)} %bitcast.1), calls=%async_computation | async-start | bytes 2097152 | tf_op jit(solution)/shard_map/all_to_all | solution.py:328
  15.1 6.6 %collective-permute-start = (s32[1,9]{1,0:T(1,128)S(1)}, s32[1,9]{1,0:T(1,128)S(1)}, u32[]{:S(2)}, u32[]{:S(2)}) collective-permute-start(s32[1,9]{1,0:T(1,128)S(1)} %pad_add_fusion.2), channel_id=1, source_target_pairs={{0,28},{4,0},{8,4},{12,8},{16,12},{20,16},{24,20},{28,24},{1,29},{... | collective-permute-start | bytes 116 | tf_op jit(solution)/shard_map/ppermute | solution.py:245
  21.8 2.8 %collective-permute-start.1 = (s32[2,9]{1,0:T(2,128)S(1)}, s32[2,9]{1,0:T(2,128)S(1)}, u32[]{:S(2)}, u32[]{:S(2)}) collective-permute-start(s32[2,9]{1,0:T(2,128)S(1)} %pad_add_fusion.1), channel_id=1, source_target_pairs={{0,24},{4,28},{8,0},{12,4},{16,8},{20,12},{24,16},{28,20},{1,25},{... | collective-permute-start | bytes 224 | tf_op jit(solution)/shard_map/ppermute | solution.py:245
  24.5 2.8 %collective-permute-start.2 = (s32[4,9]{1,0:T(4,128)S(1)}, s32[4,9]{1,0:T(4,128)S(1)}, u32[]{:S(2)}, u32[]{:S(2)}) collective-permute-start(s32[4,9]{1,0:T(4,128)S(1)} %pad_add_fusion), channel_id=1, source_target_pairs={{0,16},{4,20},{8,24},{12,28},{16,0},{20,4},{24,8},{28,12},{1,17},{... | collective-permute-start | bytes 440 | tf_op jit(solution)/shard_map/ppermute | solution.py:245

commit v4 on v3

--- a/solution.py
+++ b/solution.py
@@ -52,7 +52,9 @@
     for k in range(parts):
         at = pl.ds(k * channels, channels)
         x_copies.append(pltpu.make_async_copy(x_hbm.at[at], x.at[at], x_sem.at[k]))
-    for copy in seed_copies[1:2] + x_copies[:1] + seed_copies[3:] + x_copies[1:2] + seed_copies[:1] + x_copies[2:3] + seed_copies[2:3] + x_copies[3:]:
+    order = (1, 3, 0, 2)
+    for g, copy in zip(order, x_copies):
+        seed_copies[g].start()
         copy.start()
     coarse = QUARTER // STEP
 
@@ -65,7 +67,7 @@
             table[g, at, :GROUP] = (c * fc - s * fs).astype(jnp.bfloat16)
             table[g, at, GROUP:] = -(s * fc + c * fs).astype(jnp.bfloat16)
 
-    for g in (1, 3, 0, 2):
+    for g in order:
         fill(g)
     lanes = QUARTER
     for k, copy in enumerate(x_copies):
@@ -88,10 +90,8 @@
                 left[2 * TURN + 2 * k + 1, :, into] = (value - high.astype(jnp.float32)).astype(jnp.bfloat16)
 
     power = jnp.zeros((rows, GROUP), jnp.float32)
-    for at_g, g in enumerate((1, 3, 0, 2)):
-        if g not in (1, 3, 0, 2):
-            fill(g)
-        if at_g == 2:
+    for place, g in enumerate(order):
+        if place == 2:
             add_quarters()
         cosine, sine = table[g, :, :GROUP], table[g, :, GROUP:]
         turn = (F_LO + g) % TURN
@@ -158,41 +158,31 @@
     )(in_hbm(traces), in_hbm(jnp.asarray(seeds)))
 
 
-def cross_kernel(slots, groups, info, w, out, total):
-    owners = w.shape[0] // groups
+def cross_kernel(slots, groups, info, received, out, w, total):
+    owners = received.shape[0] // groups
     half = out.shape[1]
     lanes = 256
+    w[...] = received[...].astype(jnp.float32)
 
     def one(pair, carry):
         owner, slot = pair // slots, pair % slots
         first = pl.ds(info[owner, 2 * slot] * groups, groups)
         second = pl.ds(info[owner, 2 * slot + 1] * groups, groups)
-        alive = slot < info[owner, 2 * slots]
+        alive = jnp.where(slot < info[owner, 2 * slots], 1.0, 0.0)
         at_re = pl.ds(pl.multiple_of(pair * 16, 16), 8)
         at_im = pl.ds(pl.multiple_of(pair * 16 + 8, 8), 8)
-
-        @pl.when(alive)
-        def _():
-            for offset in range(0, half, lanes):
-                re = slice(offset, offset + lanes)
-                im = slice(half + offset, half + offset + lanes)
-                re_a, im_a = w[first, :, re].astype(jnp.float32), w[first, :, im].astype(jnp.float32)
-                re_b, im_b = w[second, :, re].astype(jnp.float32), w[second, :, im].astype(jnp.float32)
-                sum_re = jnp.sum(re_a * re_b + im_a * im_b, axis=0)
-                sum_im = jnp.sum(im_a * re_b - re_a * im_b, axis=0)
-                for k in range(0, lanes, 128):
-                    total[(offset + k) // 128, at_re, :] = sum_re[:, k : k + 128]
-                    total[(offset + k) // 128, at_im, :] = sum_im[:, k : k + 128]
-
-        @pl.when(jnp.logical_not(alive))
-        def _():
-            for k in range(half // 128):
-                total[k, at_re, :] = jnp.zeros((8, 128), jnp.float32)
-                total[k, at_im, :] = jnp.zeros((8, 128), jnp.float32)
-
+        for offset in range(0, half, lanes):
+            re = slice(offset, offset + lanes)
+            im = slice(half + offset, half + offset + lanes)
+            re_a, im_a, re_b, im_b = w[first, :, re], w[first, :, im], w[second, :, re], w[second, :, im]
+            sum_re = jnp.sum(re_a * re_b + im_a * im_b, axis=0) * alive
+            sum_im = jnp.sum(im_a * re_b - re_a * im_b, axis=0) * alive
+            for k in range(0, lanes, 128):
+                total[(offset + k) // 128, at_re, :] = sum_re[:, k : k + 128]
+                total[(offset + k) // 128, at_im, :] = sum_im[:, k : k + 128]
         return carry
 
-    lax.fori_loop(0, owners * slots, one, 0)
+    lax.fori_loop(0, owners * slots, one, 0, unroll=4)
     count = out.shape[0]
     for k in range(half // 128):
         even, odd = total[k, pl.ds(0, count, stride=2), :], total[k, pl.ds(1, count, stride=2), :]
@@ -209,7 +199,10 @@
         out_shape=jax.ShapeDtypeStruct((rows, half), jnp.bfloat16),
         in_specs=[pl.BlockSpec(memory_space=pltpu.SMEM), vmem],
         out_specs=vmem,
-        scratch_shapes=[pltpu.VMEM((half // 128, 2 * rows, 128), jnp.float32)],
+        scratch_shapes=[
+            pltpu.VMEM(received.shape, jnp.float32),
+            pltpu.VMEM((half // 128, 2 * rows, 128), jnp.float32),
+        ],
         compiler_params=pltpu.CompilerParams(vmem_limit_bytes=VMEM),
         cost_estimate=pl.CostEstimate(
             flops=8 * rows * 8 * half, bytes_accessed=2 * received.size + 2 * rows * half, transcendentals=0

time: 64.3 us -> 63.6 us (0.989)
  Pallas kernels: 12.4 us -> 11.6 us
    pallas_call x1, Pallas kernels: 2.99 us -> 2.15 us  [cross_fast(): pl.pallas_call(functools.partial(cross_kernel, slots, groups), out_shape=...]
where the time goes in v4:
time: 63.6 us; the launch traced here: 63.4 us
  waiting for transfers between devices  23.6 us (37%)
  blocking collectives  18.3 us (29%)
  Pallas kernels  11.6 us (18%)
  starting transfers between devices  8.86 us (14%)
  between operations  0.71 us (1%)
    all_to_all x1, blocking collectives, on_device(): own = lax.all_to_all(cross, AXES, split_axis=0, concat_axis=0, tiled=True)  18.3 us
    all_to_all x1, waiting for transfers between devices, on_device(): lax.all_to_all(sent, AXES, split_axis=0, concat_axis=0, tiled=True)  13.2 us
    ppermute x3, waiting for transfers between devices, every_owner(): lax.ppermute(ring, 'chan', [(source, (source - hop) % owners) for source...  10.4 us
    all_to_all x1, starting transfers between devices, on_device(): lax.all_to_all(sent, AXES, split_axis=0, concat_axis=0, tiled=True)  7.11 us
    pallas_call x1, Pallas kernels, forward(): pl.pallas_call(forward_kernel, out_shape=jax.ShapeDtypeStruct((rows, 2 *...  7.08 us
    pallas_call x1, Pallas kernels, inverse(): pl.pallas_call(functools.partial(inverse_kernel, scale), out_shape=jax.Sh...  2.35 us
    pallas_call x1, Pallas kernels, cross_fast(): pl.pallas_call(functools.partial(cross_kernel, slots, groups), out_shape=...  2.15 us
    ppermute x3, starting transfers between devices, every_owner(): lax.ppermute(ring, 'chan', [(source, (source - hop) % owners) for source...  1.76 us
  transfers between devices with their start and end apart: 4, of which 4 were waited for; matrix products, arithmetic and copies ran while one was open for 1% of the time, Pallas kernels for 0%

profile of v4, /device:TPU:1, one launch (start us, length us, event | category | flops | bytes accessed | tf_op | source)
XLA Modules:
  0.0 63.4 jit_solution(14694504274053824185)
XLA Ops:
  0.0 7.1 %forward.1 = bf16[256,2048]{1,0:T(8,128)(2,1)} custom-call(bf16[128,2,4096]{2,1,0:T(2,128)(2,1)} %x_hbm.1, f32[4,128,256]{2,1,0:T(8,128)} %constant.32.clone.seeds_hbm), custom_call_target="tpu_custom_call" | custom-call | flops 4294967296 | bytes 3145728 | tf_op jit(solution)/shard_map/forward/pallas_call | solution.py:137
  7.1 0.0 copy-start.1
  7.1 0.0 copy-start
  7.1 7.1 %all-to-all-start = ((bf16[32,8,2048]{2,1,0:T(8,128)(2,1)}), bf16[32,8,2048]{2,1,0:T(8,128)(2,1)S(1)}, u32[]{:S(2)}, u32[]{:S(2)}) async-start(bf16[32,8,2048]{2,1,0:T(8,128)(2,1)} %bitcast.1), calls=%async_computation | async-start | bytes 2097152 | tf_op jit(solution)/shard_map/all_to_all | solution.py:321
  14.9 0.0 copy-done.1
  14.9 0.1 copy.7
  15.0 0.1 reshape.15
  15.1 0.1 pad_add_fusion.2
  15.1 0.3 collective-permute-start
  15.4 6.3 %collective-permute-done = s32[1,9]{1,0:T(1,128)S(1)} collective-permute-done((s32[1,9]{1,0:T(1,128)S(1)}, s32[1,9]{1,0:T(1,128)S(1)}, u32[]{:S(2)}, u32[]{:S(2)}) %collective-permute-start) | collective-permute-done | bytes 68 | tf_op jit(solution)/shard_map/ppermute | solution.py:238
  21.8 0.2 collective-permute-start.1
  22.0 2.5 %collective-permute-done.1 = s32[2,9]{1,0:T(2,128)S(1)} collective-permute-done((s32[2,9]{1,0:T(2,128)S(1)}, s32[2,9]{1,0:T(2,128)S(1)}, u32[]{:S(2)}, u32[]{:S(2)}) %collective-permute-start.1) | collective-permute-done | bytes 104 | tf_op jit(solution)/shard_map/ppermute | solution.py:238
  24.5 1.2 %collective-permute-start.2 = (s32[4,9]{1,0:T(4,128)S(1)}, s32[4,9]{1,0:T(4,128)S(1)}, u32[]{:S(2)}, u32[]{:S(2)}) collective-permute-start(s32[4,9]{1,0:T(4,128)S(1)} %pad_add_fusion), channel_id=1, source_target_pairs={{0,16},{4,20},{8,24},{12,28},{16,0},{20,4},{24,8},{28,12},{1,17},{... | collective-permute-start | bytes 440 | tf_op jit(solution)/shard_map/ppermute | solution.py:238
  25.8 1.6 %collective-permute-done.2 = s32[4,9]{1,0:T(4,128)S(1)} collective-permute-done((s32[4,9]{1,0:T(4,128)S(1)}, s32[4,9]{1,0:T(4,128)S(1)}, u32[]{:S(2)}, u32[]{:S(2)}) %collective-permute-start.2) | collective-permute-done | bytes 176 | tf_op jit(solution)/shard_map/ppermute | solution.py:238
  27.4 13.2 %all-to-all-done.received = bf16[32,8,2048]{2,1,0:T(8,128)(2,1)S(1)} async-done(((bf16[32,8,2048]{2,1,0:T(8,128)(2,1)}), bf16[32,8,2048]{2,1,0:T(8,128)(2,1)S(1)}, u32[]{:S(2)}, u32[]{:S(2)}) %all-to-all-start) | async-done | bytes 1048608 | tf_op jit(solution)/shard_map/all_to_all | solution.py:321
  40.6 2.1 %cross.1 = bf16[256,1024]{1,0:T(8,128)(2,1)S(1)} custom-call(s32[8,9]{1,0:T(8,128)S(1)} %constant_dynamic-slice_fusion.info, bf16[32,8,2048]{2,1,0:T(8,128)(2,1)S(1)} %all-to-all-done.received), custom_call_target="tpu_custom_call" | custom-call | flops 16777216 | bytes 1572864 | tf_op jit(solution)/shard_map/cross/pallas_call | solution.py:197
  42.7 18.3 %all_to_all.10 = bf16[32,8,1024]{2,1,0:T(8,128)(2,1)S(1)} all-to-all(bf16[32,8,1024]{2,1,0:T(8,128)(2,1)S(1)} %bitcast.5), channel_id=1, replica_groups=mesh['chan'=8,'tm'=4] {'chan','tm'}, dimensions={0} | all-to-all | bytes 1048576 | tf_op jit(solution)/shard_map/all_to_all | solution.py:330
  61.0 0.0 copy-done
  61.0 2.3 %inverse.1 = f32[128,2048]{1,0:T(8,128)} custom-call(bf16[256,1024]{1,0:T(8,128)(2,1)S(1)} %bitcast.6, f32[128,1024]{1,0:T(8,128)S(1)} %copy-done), custom_call_target="tpu_custom_call" | custom-call | flops 1073741824 | bytes 1572864 | tf_op jit(solution)/shard_map/inverse/pallas_call | solution.py:283
  (4 shorter events, 0.1 us)
Async XLA Ops:
  7.1 7.8 %copy-start.1 = (s32[4,2]{0,1:T(2,128)S(1)}, s32[4,2]{0,1:T(2,128)}, u32[]{:S(2)}) copy-start(s32[4,2]{0,1:T(2,128)} %param.6) | copy-start | bytes 100
  7.1 53.9 %copy-start = (f32[128,1024]{1,0:T(8,128)S(1)}, f32[128,1024]{1,0:T(8,128)}, u32[]{:S(2)}) copy-start(f32[128,1024]{1,0:T(8,128)} %constant.33.clone.seeds) | copy-start | bytes 1572868
  7.1 33.5 %all-to-all-start = ((bf16[32,8,2048]{2,1,0:T(8,128)(2,1)}), bf16[32,8,2048]{2,1,0:T(8,128)(2,1)S(1)}, u32[]{:S(2)}, u32[]{:S(2)}) async-start(bf16[32,8,2048]{2,1,0:T(8,128)(2,1)} %bitcast.1), calls=%async_computation | async-start | bytes 2097152 | tf_op jit(solution)/shard_map/all_to_all | solution.py:321
  15.1 6.6 %collective-permute-start = (s32[1,9]{1,0:T(1,128)S(1)}, s32[1,9]{1,0:T(1,128)S(1)}, u32[]{:S(2)}, u32[]{:S(2)}) collective-permute-start(s32[1,9]{1,0:T(1,128)S(1)} %pad_add_fusion.2), channel_id=1, source_target_pairs={{0,28},{4,0},{8,4},{12,8},{16,12},{20,16},{24,20},{28,24},{1,29},{... | collective-permute-start | bytes 116 | tf_op jit(solution)/shard_map/ppermute | solution.py:238
  21.8 2.8 %collective-permute-start.1 = (s32[2,9]{1,0:T(2,128)S(1)}, s32[2,9]{1,0:T(2,128)S(1)}, u32[]{:S(2)}, u32[]{:S(2)}) collective-permute-start(s32[2,9]{1,0:T(2,128)S(1)} %pad_add_fusion.1), channel_id=1, source_target_pairs={{0,24},{4,28},{8,0},{12,4},{16,8},{20,12},{24,16},{28,20},{1,25},{... | collective-permute-start | bytes 224 | tf_op jit(solution)/shard_map/ppermute | solution.py:238
  24.5 2.8 %collective-permute-start.2 = (s32[4,9]{1,0:T(4,128)S(1)}, s32[4,9]{1,0:T(4,128)S(1)}, u32[]{:S(2)}, u32[]{:S(2)}) collective-permute-start(s32[4,9]{1,0:T(4,128)S(1)} %pad_add_fusion), channel_id=1, source_target_pairs={{0,16},{4,20},{8,24},{12,28},{16,0},{20,4},{24,8},{28,12},{1,17},{... | collective-permute-start | bytes 440 | tf_op jit(solution)/shard_map/ppermute | solution.py:238

commit v5 on v4

--- a/solution.py
+++ b/solution.py
@@ -158,11 +158,14 @@
     )(in_hbm(traces), in_hbm(jnp.asarray(seeds)))
 
 
-def cross_kernel(slots, groups, info, received, out, w, total):
+def cross_kernel(slots, groups, info_any, received, out, w, total, info, sem):
     owners = received.shape[0] // groups
     half = out.shape[1]
     lanes = 256
+    copy = pltpu.make_async_copy(info_any, info, sem)
+    copy.start()
     w[...] = received[...].astype(jnp.float32)
+    copy.wait()
 
     def one(pair, carry):
         owner, slot = pair // slots, pair % slots
@@ -182,7 +185,7 @@
                 total[(offset + k) // 128, at_im, :] = sum_im[:, k : k + 128]
         return carry
 
-    lax.fori_loop(0, owners * slots, one, 0, unroll=4)
+    lax.fori_loop(0, owners * slots, one, 0, unroll=8)
     count = out.shape[0]
     for k in range(half // 128):
         even, odd = total[k, pl.ds(0, count, stride=2), :], total[k, pl.ds(1, count, stride=2), :]
@@ -197,11 +200,13 @@
     return pl.pallas_call(
         functools.partial(cross_kernel, slots, groups),
         out_shape=jax.ShapeDtypeStruct((rows, half), jnp.bfloat16),
-        in_specs=[pl.BlockSpec(memory_space=pltpu.SMEM), vmem],
+        in_specs=[pl.BlockSpec(memory_space=pl.ANY), vmem],
         out_specs=vmem,
         scratch_shapes=[
             pltpu.VMEM(received.shape, jnp.float32),
             pltpu.VMEM((half // 128, 2 * rows, 128), jnp.float32),
+            pltpu.SMEM(info.shape, jnp.int32),
+            pltpu.SemaphoreType.DMA,
         ],
         compiler_params=pltpu.CompilerParams(vmem_limit_bytes=VMEM),
         cost_estimate=pl.CostEstimate(

time: 63.6 us -> 63.4 us (level)
  no operation moved by 1% of the time
where the time goes in v5:
time: 63.4 us; the launch traced here: 63.1 us
  waiting for transfers between devices  23.6 us (37%)
  blocking collectives  18.3 us (29%)
  Pallas kernels  11.4 us (18%)
  starting transfers between devices  8.86 us (14%)
  between operations  0.71 us (1%)
    all_to_all x1, blocking collectives, on_device(): own = lax.all_to_all(cross, AXES, split_axis=0, concat_axis=0, tiled=True)  18.3 us
    all_to_all x1, waiting for transfers between devices, on_device(): lax.all_to_all(sent, AXES, split_axis=0, concat_axis=0, tiled=True)  13.2 us
    ppermute x3, waiting for transfers between devices, every_owner(): lax.ppermute(ring, 'chan', [(source, (source - hop) % owners) for source...  10.4 us
    all_to_all x1, starting transfers between devices, on_device(): lax.all_to_all(sent, AXES, split_axis=0, concat_axis=0, tiled=True)  7.11 us
    pallas_call x1, Pallas kernels, forward(): pl.pallas_call(forward_kernel, out_shape=jax.ShapeDtypeStruct((rows, 2 *...  7.08 us
    pallas_call x1, Pallas kernels, inverse(): pl.pallas_call(functools.partial(inverse_kernel, scale), out_shape=jax.Sh...  2.35 us
    pallas_call x1, Pallas kernels, cross_fast(): pl.pallas_call(functools.partial(cross_kernel, slots, groups), out_shape=...  1.94 us
    ppermute x3, starting transfers between devices, every_owner(): lax.ppermute(ring, 'chan', [(source, (source - hop) % owners) for source...  1.76 us
  transfers between devices with their start and end apart: 4, of which 4 were waited for; matrix products, arithmetic and copies ran while one was open for 1% of the time, Pallas kernels for 0%

profile of v5, /device:TPU:1, one launch (start us, length us, event | category | flops | bytes accessed | tf_op | source)
XLA Modules:
  0.0 63.1 jit_solution(1703559075167325643)
XLA Ops:
  0.0 7.1 %forward.1 = bf16[256,2048]{1,0:T(8,128)(2,1)} custom-call(bf16[128,2,4096]{2,1,0:T(2,128)(2,1)} %x_hbm.1, f32[4,128,256]{2,1,0:T(8,128)} %constant.32.clone.seeds_hbm), custom_call_target="tpu_custom_call" | custom-call | flops 4294967296 | bytes 3145728 | tf_op jit(solution)/shard_map/forward/pallas_call | solution.py:137
  7.1 0.0 copy-start.1
  7.1 0.0 copy-start
  7.1 7.1 %all-to-all-start = ((bf16[32,8,2048]{2,1,0:T(8,128)(2,1)}), bf16[32,8,2048]{2,1,0:T(8,128)(2,1)S(1)}, u32[]{:S(2)}, u32[]{:S(2)}) async-start(bf16[32,8,2048]{2,1,0:T(8,128)(2,1)} %bitcast.1), calls=%async_computation | async-start | bytes 2097152 | tf_op jit(solution)/shard_map/all_to_all | solution.py:326
  14.9 0.0 copy-done.1
  14.9 0.1 copy.7
  15.0 0.1 reshape.15
  15.1 0.1 pad_add_fusion.2
  15.1 0.3 collective-permute-start
  15.4 6.3 %collective-permute-done = s32[1,9]{1,0:T(1,128)S(1)} collective-permute-done((s32[1,9]{1,0:T(1,128)S(1)}, s32[1,9]{1,0:T(1,128)S(1)}, u32[]{:S(2)}, u32[]{:S(2)}) %collective-permute-start) | collective-permute-done | bytes 68 | tf_op jit(solution)/shard_map/ppermute | solution.py:243
  21.8 0.2 collective-permute-start.1
  22.0 2.5 %collective-permute-done.1 = s32[2,9]{1,0:T(2,128)S(1)} collective-permute-done((s32[2,9]{1,0:T(2,128)S(1)}, s32[2,9]{1,0:T(2,128)S(1)}, u32[]{:S(2)}, u32[]{:S(2)}) %collective-permute-start.1) | collective-permute-done | bytes 104 | tf_op jit(solution)/shard_map/ppermute | solution.py:243
  24.5 1.2 %collective-permute-start.2 = (s32[4,9]{1,0:T(4,128)S(1)}, s32[4,9]{1,0:T(4,128)S(1)}, u32[]{:S(2)}, u32[]{:S(2)}) collective-permute-start(s32[4,9]{1,0:T(4,128)S(1)} %pad_add_fusion), channel_id=1, source_target_pairs={{0,16},{4,20},{8,24},{12,28},{16,0},{20,4},{24,8},{28,12},{1,17},{... | collective-permute-start | bytes 440 | tf_op jit(solution)/shard_map/ppermute | solution.py:243
  25.8 1.6 %collective-permute-done.2 = s32[4,9]{1,0:T(4,128)S(1)} collective-permute-done((s32[4,9]{1,0:T(4,128)S(1)}, s32[4,9]{1,0:T(4,128)S(1)}, u32[]{:S(2)}, u32[]{:S(2)}) %collective-permute-start.2) | collective-permute-done | bytes 176 | tf_op jit(solution)/shard_map/ppermute | solution.py:243
  27.4 13.2 %all-to-all-done.received = bf16[32,8,2048]{2,1,0:T(8,128)(2,1)S(1)} async-done(((bf16[32,8,2048]{2,1,0:T(8,128)(2,1)}), bf16[32,8,2048]{2,1,0:T(8,128)(2,1)S(1)}, u32[]{:S(2)}, u32[]{:S(2)}) %all-to-all-start) | async-done | bytes 1048608 | tf_op jit(solution)/shard_map/all_to_all | solution.py:326
  40.6 1.9 %cross.1 = bf16[256,1024]{1,0:T(8,128)(2,1)S(1)} custom-call(s32[8,9]{1,0:T(8,128)S(1)} %constant_dynamic-slice_fusion.info_any, bf16[32,8,2048]{2,1,0:T(8,128)(2,1)S(1)} %all-to-all-done.received), custom_call_target="tpu_custom_call" | custom-call | flops 16777216 | bytes 1572864 | tf_op jit(solution)/shard_map/cross/pallas_call | solution.py:200
  42.5 18.3 %all_to_all.10 = bf16[32,8,1024]{2,1,0:T(8,128)(2,1)S(1)} all-to-all(bf16[32,8,1024]{2,1,0:T(8,128)(2,1)S(1)} %bitcast.5), channel_id=1, replica_groups=mesh['chan'=8,'tm'=4] {'chan','tm'}, dimensions={0} | all-to-all | bytes 1048576 | tf_op jit(solution)/shard_map/all_to_all | solution.py:335
  60.8 0.0 copy-done
  60.8 2.4 %inverse.1 = f32[128,2048]{1,0:T(8,128)} custom-call(bf16[256,1024]{1,0:T(8,128)(2,1)S(1)} %bitcast.6, f32[128,1024]{1,0:T(8,128)S(1)} %copy-done), custom_call_target="tpu_custom_call" | custom-call | flops 1073741824 | bytes 1572864 | tf_op jit(solution)/shard_map/inverse/pallas_call | solution.py:288
  (4 shorter events, 0.1 us)
Async XLA Ops:
  7.1 7.8 %copy-start.1 = (s32[4,2]{0,1:T(2,128)S(1)}, s32[4,2]{0,1:T(2,128)}, u32[]{:S(2)}) copy-start(s32[4,2]{0,1:T(2,128)} %param.6) | copy-start | bytes 100
  7.1 53.7 %copy-start = (f32[128,1024]{1,0:T(8,128)S(1)}, f32[128,1024]{1,0:T(8,128)}, u32[]{:S(2)}) copy-start(f32[128,1024]{1,0:T(8,128)} %constant.33.clone.seeds) | copy-start | bytes 1572868
  7.1 33.5 %all-to-all-start = ((bf16[32,8,2048]{2,1,0:T(8,128)(2,1)}), bf16[32,8,2048]{2,1,0:T(8,128)(2,1)S(1)}, u32[]{:S(2)}, u32[]{:S(2)}) async-start(bf16[32,8,2048]{2,1,0:T(8,128)(2,1)} %bitcast.1), calls=%async_computation | async-start | bytes 2097152 | tf_op jit(solution)/shard_map/all_to_all | solution.py:326
  15.1 6.6 %collective-permute-start = (s32[1,9]{1,0:T(1,128)S(1)}, s32[1,9]{1,0:T(1,128)S(1)}, u32[]{:S(2)}, u32[]{:S(2)}) collective-permute-start(s32[1,9]{1,0:T(1,128)S(1)} %pad_add_fusion.2), channel_id=1, source_target_pairs={{0,28},{4,0},{8,4},{12,8},{16,12},{20,16},{24,20},{28,24},{1,29},{... | collective-permute-start | bytes 116 | tf_op jit(solution)/shard_map/ppermute | solution.py:243
  21.8 2.8 %collective-permute-start.1 = (s32[2,9]{1,0:T(2,128)S(1)}, s32[2,9]{1,0:T(2,128)S(1)}, u32[]{:S(2)}, u32[]{:S(2)}) collective-permute-start(s32[2,9]{1,0:T(2,128)S(1)} %pad_add_fusion.1), channel_id=1, source_target_pairs={{0,24},{4,28},{8,0},{12,4},{16,8},{20,12},{24,16},{28,20},{1,25},{... | collective-permute-start | bytes 224 | tf_op jit(solution)/shard_map/ppermute | solution.py:243
  24.5 2.8 %collective-permute-start.2 = (s32[4,9]{1,0:T(4,128)S(1)}, s32[4,9]{1,0:T(4,128)S(1)}, u32[]{:S(2)}, u32[]{:S(2)}) collective-permute-start(s32[4,9]{1,0:T(4,128)S(1)} %pad_add_fusion), channel_id=1, source_target_pairs={{0,16},{4,20},{8,24},{12,28},{16,0},{20,4},{24,8},{28,12},{1,17},{... | collective-permute-start | bytes 440 | tf_op jit(solution)/shard_map/ppermute | solution.py:243
